TPU v7x, 32 devices: a whole 2x2x4 slice. The times are simulated.
32 devices in a mesh: groups: 2 (over x), seq: 16 (over z, y, core).
Axes of the slice: x: 2, y: 2, z: 4, core: 2. Of those that a mesh axis runs over, the one named last changes fastest.
Arguments:
- queries: bfloat16 [16384, 2048], P(('groups', 'seq')), parts along dimension 0, may hold values from -10 to 10
- keys: bfloat16 [16384, 2048], P(('groups', 'seq')), parts along dimension 0, may hold values from -10 to 10
- values: bfloat16 [16384, 2048], P(('groups', 'seq')), parts along dimension 0, may hold values from -6 to 6
- ssd_input: bfloat16 [16384, 2048], P(('groups', 'seq')), parts along dimension 0, may hold values from -6 to 6
- bmat: bfloat16 [16384, 128], P(('groups', 'seq')), parts along dimension 0, may hold values from -0.5 to 0.5
- cmat: bfloat16 [16384, 128], P(('groups', 'seq')), parts along dimension 0, may hold values from -6 to 6
- expo: int32 [16384, 32], P(('groups', 'seq')), parts along dimension 0, may hold values from 1 to 16384
- rate: float32 [32], replicated, may hold values from 1.2207031e-05 to 0.06
- skip: float32 [32], replicated, may hold values from 0.5 to 1.5
Outputs:
- attn_out: bfloat16 [16384, 2048], P(('groups', 'seq')), parts along dimension 0
- normed_recurrence_output: bfloat16 [16384, 2048], P(('groups', 'seq')), parts along dimension 0
There are 2 independent parts, one for each index of `groups`. A program takes and returns all parts, laid end to end along the dimension named above; an argument that names none is the same for every part. Nothing has to cross between parts.
All inputs are finite; a program needn't handle non-finite values.
Results may differ from a plain program's by a relative error of at most 0.0049.
Values may be sent and summed in bfloat16 or wider, within the bound.
A program may use at most 192 MiB of HBM per device.

v0:
```python
import functools
import math

import jax
import jax.numpy as jnp
from jax import lax
from jax.experimental import pallas as pl
from jax.experimental.pallas import tpu as pltpu
from jax.sharding import PartitionSpec as P

E = 128
W = 2048
Q = 256
CHUNK = 256
NEG = -1e30
LOG2E = math.log2(math.e)
MESH = pl.DeviceIdType.MESH
Z, Y, A, B = range(4)


def dot(a, b):
    return jnp.dot(a, b, preferred_element_type=jnp.float32)


def dot_t(a, b):
    return lax.dot_general(a, b, (((1,), (1,)), ((), ())), preferred_element_type=jnp.float32)


def attend(bias, q_ref, ko_ref, vo_ref, held, out_ref, chunk):
    length = q_ref.shape[0]
    tq = min(256, length)
    scale = LOG2E / math.sqrt(E)
    row = lax.broadcasted_iota(jnp.int32, (tq, tq), 0)
    col = lax.broadcasted_iota(jnp.int32, (tq, tq), 1)
    for head in range(CHUNK // E):
        wide = pl.ds(pl.multiple_of(chunk * CHUNK + head * E, E), E)
        near = slice(head * E, (head + 1) * E)
        for r in range(0, length, tq):
            q = q_ref[r : r + tq, wide]
            tiles = [(None, r, tq, "low")]
            if r > 0:
                tiles.append((None, 0, r, None))
            tiles.append((Z, r, tq, "up"))
            if r + tq < length:
                tiles.append((Z, r + tq, length - r - tq, None))
            tiles += [(n, 0, length, None) for n in (Y, A, B)]
            m = l = acc = None
            for kind, start, size, mask in tiles:
                rows = slice(start, start + size)
                if kind is None:
                    k, v = ko_ref[rows, wide], vo_ref[rows, wide]
                else:
                    k, v = held[kind, chunk, 0, rows, near], held[kind, chunk, 1, rows, near]
                s = dot_t(q, k) * scale
                if mask == "low":
                    s = jnp.where(col <= row, s, NEG)
                elif mask == "up":
                    s = jnp.where(col > row, s, NEG)
                peak = jnp.max(s, axis=1, keepdims=True)
                if kind is not None:
                    peak = peak + bias[kind]
                m_new = peak if m is None else jnp.maximum(m, peak)
                shift = m_new if kind is None else m_new - bias[kind]
                p = jnp.exp2(s - shift)
                total = jnp.sum(p, axis=1, keepdims=True)
                part = dot(p.astype(jnp.bfloat16), v)
                if m is None:
                    l, acc = total, part
                else:
                    alpha = jnp.exp2(m - m_new)
                    l = l * alpha + total
                    acc = acc * alpha + part
                m = m_new
            out_ref[r : r + tq, wide] = (acc / l).astype(out_ref.dtype)


def pair_columns(lane, table, j, width):
    return jnp.where(lane < width, table[:, 2 * j : 2 * j + 1], table[:, 2 * j + 1 : 2 * j + 2])


def local_states(x_ref, bt_ref, end_ref, decay_ref, local, total):
    rows, total_cols = x_ref.shape
    head_count = end_ref.shape[1]
    width = total_cols // head_count
    lane = lax.broadcasted_iota(jnp.int32, (1, 2 * width), 1)
    weights = jnp.exp(end_ref[...])
    for j in range(head_count // 2):
        cs = slice(2 * width * j, 2 * width * (j + 1))
        state = None
        for block in range(rows // Q):
            rs = slice(block * Q, (block + 1) * Q)
            xs = x_ref[rs, cs].astype(jnp.float32) * pair_columns(lane, weights[rs], j, width)
            one = dot(bt_ref[:, rs], xs.astype(jnp.bfloat16))
            local[block, :, cs] = one
            state = one if state is None else state * decay_ref[block : block + 1, cs] + one
        total[:, cs] = state.astype(jnp.bfloat16)


def recurrence(block, x_ref, b_ref, c_ref, cum_ref, cumt_ref, skip_ref, carried_ref, local, decay_ref, out_ref):
    rows, total_cols = x_ref.shape
    head_count = cum_ref.shape[1]
    width = total_cols // head_count
    pair = 2 * width
    lane = lax.broadcasted_iota(jnp.int32, (1, pair), 1)
    low = lax.broadcasted_iota(jnp.int32, (Q, Q), 1) <= lax.broadcasted_iota(jnp.int32, (Q, Q), 0)
    same = (lax.broadcasted_iota(jnp.int32, (pair, pair), 0) < width) == (
        lax.broadcasted_iota(jnp.int32, (pair, pair), 1) < width
    )
    ones = jnp.where(same, 1.0, 0.0).astype(jnp.bfloat16)
    rs = slice(block * Q, (block + 1) * Q)
    c = c_ref[rs, :]
    cross = jnp.where(low, dot_t(c, b_ref[rs, :]), 0.0)
    cum = cum_ref[rs, :]
    grown = jnp.exp(cum)
    for j in range(head_count // 2):
        cs = slice(pair * j, pair * (j + 1))
        x = x_ref[rs, cs]
        intra = []
        for h in (2 * j, 2 * j + 1):
            gap = cum[:, h : h + 1] - cumt_ref[h : h + 1, rs]
            grid = jnp.exp(jnp.minimum(gap, 0.0))
            intra.append(dot((cross * grid).astype(jnp.bfloat16), x))
        carried = carried_ref[:, cs].astype(jnp.float32)
        for b in range(block):
            carried = carried * decay_ref[b : b + 1, cs] + local[b, :, cs]
        high = carried.astype(jnp.bfloat16)
        inter = dot(c, high)
        if block:
            inter = inter + dot(c, (carried - high.astype(jnp.float32)).astype(jnp.bfloat16))
        mixed = (
            jnp.where(lane < width, intra[0], intra[1])
            + inter * pair_columns(lane, grown, j, width)
            + skip_ref[:, cs] * x.astype(jnp.float32)
        )
        square = mixed * mixed
        big = square.astype(jnp.bfloat16)
        small = (square - big.astype(jnp.float32)).astype(jnp.bfloat16)
        mean = (dot(big, ones) + dot(small, ones)) * (1.0 / width)
        out_ref[rs, cs] = (mixed * lax.rsqrt(mean + 1e-05)).astype(out_ref.dtype)


def kernel(
    size, q_ref, k_ref, v_ref, x_ref, b_ref, bt_ref, c_ref, cum_ref, cumt_ref, end_ref, decay_ref,
    dev_ref, skip_ref, attn_ref, rec_ref, held, local, total, got_s, got_d, sum_q, dec_q, far_s,
    far_d, parts, carried, send, recv, send1, recv1, send2, recv2, send3, recv3,
):
    quads = size // 4
    here = lax.axis_index("seq")
    mine = lax.axis_index("groups")
    quad = here // 4
    member = here % 4
    row = member // 2
    core = member % 2
    chunks = k_ref.shape[1] // CHUNK
    group = total.shape[1] // 4
    blocks = x_ref.shape[0] // Q

    def other(d):
        return 2 * (1 - row if d // 2 else row) + (1 - core if d % 2 else core)

    def beside(d):
        return (mine, quad * 4 + other(d))

    def beyond(e):
        return (mine, (quad + e) % quads * 4 + member)

    def copy(src, dst, sender, receiver, device):
        return pltpu.make_async_remote_copy(
            src_ref=src, dst_ref=dst, send_sem=sender, recv_sem=receiver,
            device_id=device, device_id_type=MESH,
        )

    barrier = pltpu.get_barrier_semaphore()
    for d in range(1, 4):
        pl.semaphore_signal(barrier, inc=1, device_id=beside(d), device_id_type=MESH)
    for e in range(1, quads):
        pl.semaphore_signal(barrier, inc=1, device_id=beyond(e), device_id_type=MESH)
    pl.semaphore_wait(barrier, 3 + quads - 1)

    target = {Z: beyond(1), Y: beside(2), A: beside(1), B: beside(1)}

    def move(kind, chunk, part, src):
        return copy(
            src, held.at[kind, chunk, part], send.at[kind, chunk, part],
            recv.at[kind, chunk, part], target[kind],
        )

    def send_own(kind, chunk):
        wide = pl.ds(pl.multiple_of(chunk * CHUNK, CHUNK), CHUNK)
        for part, ref in ((0, k_ref), (1, v_ref)):
            move(kind, chunk, part, ref.at[:, wide]).start()

    def pass_on(kind, chunk, source):
        for part in range(2):
            move(kind, chunk, part, held.at[source, chunk, part]).start()

    def arrived(kind, chunk):
        for part in range(2):
            move(kind, chunk, part, held.at[kind, chunk, part]).wait_recv()

    def offer(chunk):
        send_own(Z, chunk)

        @pl.when(core == 0)
        def _():
            send_own(B, chunk)

    def relay(chunk):
        @pl.when(row == 0)
        def _():
            send_own(Y, chunk)

        arrived(Z, chunk)

        @pl.when(row == 1)
        def _():
            pass_on(Y, chunk, Z)

        @pl.when(core == 1)
        def _():
            pass_on(B, chunk, Z)

    ahead = 2 - core
    offer(0)

    @pl.when(core == 0)
    def _():
        offer(1)

    def columns(which):
        return pl.ds(pl.multiple_of(which * group, group), group)

    local_states(x_ref, bt_ref, end_ref, decay_ref, local, total)

    def to_member(d):
        at = columns(other(d))
        return (
            copy(total.at[:, at], got_s.at[d], send1.at[0, d], recv1.at[0, d], beside(d)),
            copy(dev_ref.at[:, at], got_d.at[d], send1.at[1, d], recv1.at[1, d], beside(d)),
        )

    def to_quad(e):
        return (
            copy(sum_q, far_s.at[e], send2.at[0, e], recv2.at[0, e], beyond(e)),
            copy(dec_q, far_d.at[e], send2.at[1, e], recv2.at[1, e], beyond(e)),
        )

    def to_owner(d):
        return copy(
            parts.at[other(d)], carried.at[:, columns(member)], send3.at[d], recv3.at[d], beside(d)
        )

    for d in range(1, 4):
        for one in to_member(d):
            one.start()
    got_s[0] = total[:, columns(member)]
    got_d[0] = dev_ref[:, columns(member)]
    for d in range(1, 4):
        for one in to_member(d):
            one.wait_recv()

    def slot(j):
        return jnp.abs(j // 2 - row) * 2 + jnp.abs(j % 2 - core)

    def state_of(j):
        return got_s[slot(j)].astype(jnp.float32)

    def decay_of(j):
        return got_d[slot(j)]

    sums = state_of(0)
    decays = decay_of(0)
    for j in range(1, 4):
        sums = sums * decay_of(j)[0:1] + state_of(j)
        decays = decays * decay_of(j)
    sum_q[...] = sums.astype(jnp.bfloat16)
    dec_q[...] = decays
    for e in range(1, quads):
        for one in to_quad(e):
            one.start()

    def spread():
        for e in range(1, quads):
            for one in to_quad(e):
                one.wait_recv()
        entry = jnp.zeros(sum_q.shape, jnp.float32)
        for e in range(quads - 1, 0, -1):
            grown = entry * far_d[e][0:1] + far_s[e].astype(jnp.float32)
            entry = jnp.where(quad >= e, grown, entry)
        for j in range(4):
            parts[j] = entry.astype(jnp.bfloat16)
            if j < 3:
                entry = entry * decay_of(j)[0:1] + state_of(j)
        for d in range(1, 4):
            to_owner(d).start()
        carried[:, columns(member)] = parts[member]

    def finish(block):
        recurrence(
            block, x_ref, b_ref, c_ref, cum_ref, cumt_ref, skip_ref, carried, local, decay_ref, rec_ref
        )

    def off(seen):
        return jnp.where(seen, 0.0, NEG).astype(jnp.float32)

    inside = quad > 0
    bias = {
        Z: off(inside),
        Y: off(inside | (row == 1)),
        A: off(inside | (row == 1)),
        B: off(inside | (core == 1)),
    }

    relay(0)
    offer(ahead)

    def step(j, carry):
        @pl.when(j + 1 < chunks)
        def _():
            relay(j + 1)

        @pl.when(j + 1 + ahead < chunks)
        def _():
            offer(j + 1 + ahead)

        @pl.when(j < chunks)
        def _():
            arrived(Y, j)
            pass_on(A, j, Y)

        @pl.when(j > 0)
        def _():
            arrived(A, j - 1)
            arrived(B, j - 1)
            attend(bias, q_ref, k_ref, v_ref, held, attn_ref, j - 1)

        @pl.when(j == 2)
        def _():
            spread()

        for block in range(blocks):

            @pl.when(j == min(4 + block, chunks))
            def _():
                if block == 0:
                    for d in range(1, 4):
                        copy(
                            parts.at[other(d)], carried.at[:, columns(other(d))], send3.at[d],
                            recv3.at[d], beside(d),
                        ).wait_recv()
                finish(block)

        return carry

    lax.fori_loop(0, chunks + 1, step, 0)

    for d in range(1, 4):
        for one in to_member(d):
            one.wait_send()
        to_owner(d).wait_send()
    for e in range(1, quads):
        for one in to_quad(e):
            one.wait_send()

    def drain(j, carry):
        for kind in range(4):
            for part in range(2):
                move(kind, j, part, held.at[kind, j, part]).wait_send()
        return carry

    lax.fori_loop(0, chunks, drain, 0)


def on_device(queries, keys, values, ssd_input, bmat, cmat, expo, rate, skip):
    length, total_cols = queries.shape
    size = lax.axis_size("seq")
    head_count = rate.shape[0]
    x_cols = ssd_input.shape[1]
    width = x_cols // head_count
    blocks = length // Q
    state = cmat.shape[1]
    group = x_cols // 4
    quads = size // 4
    chunks = total_cols // CHUNK

    loga = -rate[None, :] * expo.astype(jnp.float32)
    cum3 = jnp.cumsum(loga.reshape(blocks, Q, head_count), axis=1)
    ends = cum3[:, -1, :]
    cum = cum3.reshape(length, head_count)
    end_gap = (ends[:, None, :] - cum3).reshape(length, head_count)
    decay_cols = jnp.repeat(jnp.exp(ends), width, axis=1)
    dev = jnp.broadcast_to(jnp.prod(decay_cols, axis=0, keepdims=True), (8, x_cols))
    args = (
        queries, keys, values, ssd_input, bmat, bmat.T, cmat, cum, cum.T, end_gap, decay_cols, dev,
        jnp.repeat(skip, width)[None, :],
    )
    vmem = pl.BlockSpec(memory_space=pltpu.VMEM)
    dma = pltpu.SemaphoreType.DMA
    return pl.pallas_call(
        functools.partial(kernel, size),
        in_specs=[vmem] * len(args),
        out_specs=(vmem, vmem),
        out_shape=(
            jax.ShapeDtypeStruct(queries.shape, jnp.bfloat16),
            jax.ShapeDtypeStruct(ssd_input.shape, jnp.bfloat16),
        ),
        scratch_shapes=[
            pltpu.VMEM((4, chunks, 2, length, CHUNK), jnp.bfloat16),
            pltpu.VMEM((blocks, state, x_cols), jnp.float32),
            pltpu.VMEM((state, x_cols), jnp.bfloat16),
            pltpu.VMEM((4, state, group), jnp.bfloat16),
            pltpu.VMEM((4, 8, group), jnp.float32),
            pltpu.VMEM((state, group), jnp.bfloat16),
            pltpu.VMEM((8, group), jnp.float32),
            pltpu.VMEM((quads, state, group), jnp.bfloat16),
            pltpu.VMEM((quads, 8, group), jnp.float32),
            pltpu.VMEM((4, state, group), jnp.bfloat16),
            pltpu.VMEM((state, x_cols), jnp.bfloat16),
            dma((4, chunks, 2)),
            dma((4, chunks, 2)),
            dma((2, 4)),
            dma((2, 4)),
            dma((2, quads)),
            dma((2, quads)),
            dma((4,)),
            dma((4,)),
        ],
        compiler_params=pltpu.CompilerParams(
            collective_id=0, has_side_effects=True, vmem_limit_bytes=58 << 20
        ),
        name="attention_and_recurrence",
    )(*args)


def solution(mesh):
    split = P(("groups", "seq"), None)
    return jax.shard_map(
        on_device,
        mesh=mesh,
        in_specs=(split,) * 7 + (P(), P()),
        out_specs=(split, split),
        check_vma=False,
    )
```

profile of v0, /device:TPU:9, one launch (start us, length us, event | category | flops | bytes accessed | tf_op | source)
XLA Modules:
  0.0 188.2 jit_solution(11633539060858924735)
XLA Ops:
  0.6 0.7 neg.4
  1.3 0.7 broadcast_in_dim.18
  2.0 0.7 broadcast_in_dim_reshape.3.skip_ref
  2.7 0.9 convert_multiply_fusion
  3.6 1.2 reduce-window.6
  4.8 0.2 slice_reduce_fusion
  5.0 1.7 copy.22
  6.7 0.1 bitcast_bitcast_fusion.1
  6.7 0.2 slice_reduce_fusion.1
  6.9 0.1 broadcast_subtract_fusion
  7.0 0.1 reduce_prod.12
  7.1 0.1 broadcast_in_dim.16
  7.2 0.1 broadcast_in_dim.15
  7.3 0.7 reshape.36.decay_ref
  7.9 0.6 broadcast_in_dim.17.dev_ref
  8.6 0.0 copy-start.1
  8.6 0.8 copy.27
  9.4 0.8 copy.28.cum_ref
  10.2 0.0 copy-done.1
  10.3 173.3 %attention_and_recurrence.1 = (bf16[512,2048]{1,0:T(8,128)(2,1)}, bf16[512,2048]{1,0:T(8,128)(2,1)}) custom-call(bf16[512,2048]{1,0:T(8,128)(2,1)} %q_ref.1, bf16[512,2048]{1,0:T(8,128)(2,1)} %k_ref.1, bf16[512,2048]{1,0:T(8,128)(2,1)} %v_ref.1, bf16[512,2048]{1,0:T(8,128)(2,1)} %x_ref.1, bf16[512,128]{1,0:T(8,128)(2,1)} %b_ref.1, ...), custom_call_target="tpu_custom_call" | custom-call | tf_op jit(solution)/shard_map/attention_and_recurrence/pallas_call | solution.py:399
  183.6 0.0 copy-start
  183.6 3.3 %copy.42 = bf16[512,2048]{1,0:T(8,128)(2,1)} copy(bf16[512,2048]{1,0:T(8,128)(2,1)} %get-tuple-element.8) | data formatting | bytes 4194304
  186.9 0.0 copy-done
  186.9 1.3 copy.43
  (5 shorter events, 0.1 us)
Async XLA Ops:
  8.6 1.7 copy-start.1
  183.6 3.3 %copy-start = (bf16[512,2048]{1,0:T(8,128)(2,1)S(1)}, bf16[512,2048]{1,0:T(8,128)(2,1)}, u32[]{:S(2)}) copy-start(bf16[512,2048]{1,0:T(8,128)(2,1)} %get-tuple-element.9) | copy-start | bytes 6291460
where the time goes:
time: 189 us; the launch traced here: 188 us
  Pallas kernels  173 us (92%)
  local copies, waits for them, and re-layouts  11.2 us (6%)
  other arithmetic  2.98 us (2%)
    pallas_call x1, Pallas kernels, on_device(): pl.pallas_call(functools.partial(kernel, size), in_specs=[vmem] * len(arg...  173 us
    unnamed x7, local copies, waits for them, and re-layouts  6.29 us

commit v1 on v0

v1 whole, which is shorter than its diff:
```python
import functools
import math

import jax
import jax.numpy as jnp
from jax import lax
from jax.experimental import pallas as pl
from jax.experimental.pallas import tpu as pltpu
from jax.sharding import PartitionSpec as P

E = 128
Q = 256
LANES = 128
NEG = -1e30
LOG2E = math.log2(math.e)
MESH = pl.DeviceIdType.MESH
Z, Y, A, B = range(4)
BF16 = jnp.bfloat16
F32 = jnp.float32


def dot(a, b):
    return jnp.dot(a, b, preferred_element_type=F32)


def dot_t(a, b):
    return lax.dot_general(a, b, (((1,), (1,)), ((), ())), preferred_element_type=F32)


def iota(shape, axis):
    return lax.broadcasted_iota(jnp.int32, shape, axis)


def split(a):
    high = a.astype(BF16)
    rest = a - high.astype(F32)
    middle = rest.astype(BF16)
    return high, middle, (rest - middle.astype(F32)).astype(BF16)


def table(a):
    parts = split(a)
    rest = jnp.zeros((a.shape[0], LANES - 3 * a.shape[1]), BF16)
    return jnp.concatenate([*parts, rest], axis=1)


def wide(a):
    return jnp.concatenate([a, jnp.zeros((a.shape[0], LANES - a.shape[1]), F32)], axis=1)


def lanes_of(j):
    return pl.ds(pl.multiple_of(j * LANES, LANES), LANES)


def flash(q, tiles, m, l, acc):
    tq = q.shape[0]
    scale = LOG2E / math.sqrt(E)
    for k, v, bias, mask in tiles:
        s = dot_t(q, k) * scale
        if mask is not None:
            row, col = iota((tq, tq), 0), iota((tq, tq), 1)
            s = jnp.where(col <= row if mask == "low" else col > row, s, NEG)
        peak = jnp.max(s, axis=1, keepdims=True)
        if bias is not None:
            peak = peak + bias
        m_new = peak if m is None else jnp.maximum(m, peak)
        shift = m_new if bias is None else m_new - bias
        p = jnp.exp2(s - shift)
        total = jnp.sum(p, axis=1, keepdims=True)
        part = dot(p.astype(BF16), v)
        if m is None:
            l, acc = total, part
        else:
            alpha = jnp.exp2(m - m_new)
            l = l * alpha + total
            acc = acc * alpha + part
        m = m_new
    return m, l, acc


def kernel(
    size, q_in, k_in, v_in, x_in, b_in, c_in, expo_in, rate_ref, skip_ref, attn_ref, rec_ref,
    q_ref, k_ref, v_ref, x_ref, b_ref, c_ref, expo_ref, held, hot, t3, cumt, bt, cross, dec, skx,
    dl, dtab, local, tot, s1, tc, s2, ein, eout, s4out, ec, s5out, carried, mixed, acc_ref, ml_ref,
    load, send, recv, dl_send, dl_recv, s1_send, s1_recv, s5_send, s5_recv, one_send, one_recv,
):
    nz = size // 4
    here = lax.axis_index("seq")
    mine = lax.axis_index("groups")
    z = here // 4
    member = here % 4
    row = member // 2
    core = member % 2
    length, total_cols = q_ref.shape
    x_cols = x_ref.shape[1]
    heads = total_cols // E
    pairs = x_cols // LANES
    head_count = rate_ref.shape[1]
    width = x_cols // head_count
    group = x_cols // 4
    blocks = length // Q
    tq = min(256, length)
    has_z = z > 0
    has_next = z < nz - 1
    has_y = has_z | (row == 1)
    has_b = has_z | (core == 1)

    def beside(d):
        r = 1 - row if d // 2 else row
        c = 1 - core if d % 2 else core
        return (mine, z * 4 + 2 * r + c)

    def beyond(step):
        return (mine, (z + step + nz) % nz * 4 + member)

    def copy(src, dst, sender, receiver, device):
        return pltpu.make_async_remote_copy(
            src_ref=src, dst_ref=dst, send_sem=sender, recv_sem=receiver,
            device_id=device, device_id_type=MESH,
        )

    inputs = (
        (expo_in, expo_ref), (b_in, b_ref), (c_in, c_ref), (x_in, x_ref), (q_in, q_ref),
        (k_in, k_ref), (v_in, v_ref),
    )
    loads = [pltpu.make_async_copy(a, b, load.at[i]) for i, (a, b) in enumerate(inputs)]
    for one in loads[:4]:
        one.start()

    barrier = pltpu.get_barrier_semaphore()
    for d in range(1, 4):
        pl.semaphore_signal(barrier, inc=1, device_id=beside(d), device_id_type=MESH)

    @pl.when(has_z)
    def _():
        pl.semaphore_signal(barrier, inc=1, device_id=beyond(-1), device_id_type=MESH)

    @pl.when(has_next)
    def _():
        pl.semaphore_signal(barrier, inc=1, device_id=beyond(1), device_id_type=MESH)

    pl.semaphore_wait(barrier, 3 + jnp.minimum(z, 1) + jnp.minimum(nz - 1 - z, 1))

    target = {Z: beyond(1), Y: beside(2), A: beside(1), B: beside(1)}

    def send_own(kind, h):
        for part, ref in ((0, k_in), (1, v_in)):
            copy(
                ref.at[:, lanes_of(h)], held.at[kind, h, part], send.at[kind, h], recv.at[kind, h],
                target[kind],
            ).start()

    def whole(kind, h, source):
        return copy(
            held.at[source, h], held.at[kind, h], send.at[kind, h], recv.at[kind, h], target[kind]
        )

    def arrived(kind, h):
        whole(kind, h, kind).wait_recv()

    def sent(kind, h):
        whole(kind, h, kind).wait_send()

    def offer(h):
        @pl.when(has_next)
        def _():
            send_own(Z, h)

        @pl.when(row == 0)
        def _():
            send_own(Y, h)

        @pl.when(core == 0)
        def _():
            send_own(B, h)

    offer(0)
    offer(1)
    for one in loads[4:]:
        one.start()

    def own_dl(d):
        return copy(dl.at[0], dl.at[d], dl_send.at[d], dl_recv.at[d], beside(d))

    def quarter(u, c):
        return pl.ds(pl.multiple_of((2 * u + c) * group, group), group)

    def to_core(u):
        return copy(
            tot.at[:, quarter(u, 1 - core)], s1.at[u], s1_send.at[u], s1_recv.at[u], beside(1)
        )

    def to_row():
        return copy(tc.at[1 - row], s2, one_send.at[0], one_recv.at[0], beside(2))

    def to_next():
        return copy(eout, ein, one_send.at[1], one_recv.at[1], beyond(1))

    def back_row():
        return copy(s4out, ec.at[row], one_send.at[2], one_recv.at[2], beside(2))

    def back_core(u):
        return copy(
            s5out.at[u], carried.at[:, quarter(u, core)], s5_send.at[u], s5_recv.at[u], beside(1)
        )

    ki = iota((LANES, x_cols), 0)
    hi = lax.div(iota((LANES, x_cols), 1), width)
    match = ki == hi
    for p in (1, 2):
        match = match | (ki - p * head_count == hi)
    hot[...] = jnp.where(match, 1.0, 0.0).astype(BF16)

    @pl.when(z == 0)
    def _():
        ein[...] = jnp.zeros_like(ein)

    low = iota((Q, Q), 1) <= iota((Q, Q), 0)
    upto = jnp.where(iota((Q, Q), 0) <= iota((Q, Q), 1), 1.0, 0.0).astype(BF16)
    loads[0].wait()
    rates = wide(rate_ref[...])[0:1, :]
    rates = jnp.broadcast_to(rates, (LANES, LANES)).T[0:head_count, 0:1]
    dlog = None
    for b in range(blocks):
        rs = slice(b * Q, (b + 1) * Q)
        loga = -rates * expo_ref[:, rs].astype(F32)
        sums = sum(dot(part, upto) for part in split(loga))
        cumt[:, rs] = sums
        rest = jnp.zeros((LANES - head_count, Q), F32)
        cum = jnp.concatenate([sums, rest], axis=0).T[:, 0:head_count]
        t3[rs, :] = table(cum)
        last = cum[Q - 1 :, :]
        dlog = last if dlog is None else dlog + last
    dl[0] = jnp.broadcast_to(wide(dlog), dl.shape[1:])
    for d in range(1, 4):
        own_dl(d).start()
    skx[...] = jnp.broadcast_to(dot(table(skip_ref[...]), hot[...]), skx.shape)
    loads[1].wait()
    loads[2].wait()
    bt[...] = b_ref[...].astype(F32).T.astype(BF16)
    for b in range(blocks):
        rs = slice(b * Q, (b + 1) * Q)
        cross[b] = jnp.where(low, dot_t(c_ref[rs, :], b_ref[rs, :]), 0.0)
    loads[3].wait()

    lane = iota((1, LANES), 1)

    def spread(rs, cs):
        return dot(t3[rs, :], hot[:, cs])

    def local_state(j, carry):
        cs = lanes_of(j)
        state = None
        for b in range(blocks):
            rs = slice(b * Q, (b + 1) * Q)
            cum = spread(rs, cs)
            end = cum[Q - 1 :, :]
            xs = x_ref[rs, cs].astype(F32) * jnp.exp(end - cum)
            one = dot(bt[:, rs], xs.astype(BF16))
            grown = jnp.exp(end)
            local[b, :, cs] = one
            dec[b : b + 1, cs] = grown
            state = one if state is None else state * grown + one
        tot[:, cs] = state.astype(BF16)
        return carry

    def intra(j, carry):
        cs = lanes_of(j)
        for b in range(blocks):
            rs = slice(b * Q, (b + 1) * Q)
            cum = spread(rs, cs)
            x = x_ref[rs, cs]
            both = []
            for a in range(2):
                gap = cum[:, a * width : a * width + 1] - cumt[pl.ds(2 * j + a, 1), rs]
                grid = jnp.exp(jnp.minimum(gap, 0.0))
                both.append(dot((cross[b] * grid).astype(BF16), x))
            mixed[rs, cs] = (
                jnp.where(lane < width, both[0], both[1]) + skx[0:1, cs] * x.astype(F32)
            )
        return carry

    same = (iota((LANES, LANES), 0) < width) == (iota((LANES, LANES), 1) < width)
    ones = jnp.where(same, 1.0, 0.0).astype(BF16)

    def finish(j, carry):
        cs = lanes_of(j)
        entry = carried[:, cs].astype(F32)
        for b in range(blocks):
            rs = slice(b * Q, (b + 1) * Q)
            c = c_ref[rs, :]
            high = entry.astype(BF16)
            inter = dot(c, high)
            if b:
                inter = inter + dot(c, (entry - high.astype(F32)).astype(BF16))
            value = mixed[rs, cs] + inter * jnp.exp(spread(rs, cs))
            square = value * value
            big = square.astype(BF16)
            small = (square - big.astype(F32)).astype(BF16)
            mean = (dot(big, ones) + dot(small, ones)) * (1.0 / width)
            rec_ref[rs, cs] = (value * lax.rsqrt(mean + 1e-05)).astype(rec_ref.dtype)
            if b + 1 < blocks:
                entry = entry * dec[b : b + 1, cs] + local[b, :, cs]
        return carry

    def off(seen):
        return jnp.where(seen, 0.0, NEG).astype(F32)

    bias = {Z: off(has_z), Y: off(has_y), A: off(has_y), B: off(has_b)}

    def first_part(h):
        hs = lanes_of(h)
        for r in range(0, length, tq):
            rows = slice(r, r + tq)
            tiles = [(k_ref[rows, hs], v_ref[rows, hs], None, "low")]
            if r > 0:
                tiles.append((k_ref[0:r, hs], v_ref[0:r, hs], None, None))
            tiles.append((held[Z, h, 0, rows, :], held[Z, h, 1, rows, :], bias[Z], "up"))
            if r + tq < length:
                past = slice(r + tq, length)
                tiles.append((held[Z, h, 0, past, :], held[Z, h, 1, past, :], bias[Z], None))
            tiles.append((held[B, h, 0], held[B, h, 1], bias[B], None))
            m, l, acc = flash(q_ref[rows, hs], tiles, None, None, None)
            acc_ref[rows, :] = acc
            ml_ref[0, rows, :] = jnp.broadcast_to(m, acc.shape)
            ml_ref[1, rows, :] = jnp.broadcast_to(l, acc.shape)

    def second_part(h):
        hs = lanes_of(h)
        for r in range(0, length, tq):
            rows = slice(r, r + tq)
            tiles = [(held[n, h, 0], held[n, h, 1], bias[n], None) for n in (Y, A)]
            m, l, acc = flash(
                q_ref[rows, hs], tiles, ml_ref[0, rows, 0:1], ml_ref[1, rows, 0:1], acc_ref[rows, :]
            )
            attn_ref[rows, hs] = (acc / l).astype(attn_ref.dtype)

    @pl.when(z == 0)
    def _():
        def clear(h, carry):
            held[Z, h] = jnp.zeros(held.shape[2:], BF16)

            @pl.when(row == 0)
            def _():
                held[Y, h] = jnp.zeros(held.shape[2:], BF16)
                held[A, h] = jnp.zeros(held.shape[2:], BF16)

            @pl.when(core == 0)
            def _():
                held[B, h] = jnp.zeros(held.shape[2:], BF16)

            return carry

        lax.fori_loop(0, heads, clear, 0)

    def chip_totals():
        for d in range(1, 4):
            own_dl(d).wait_recv()
        which = iota((8, LANES), 0)
        rows = sum(jnp.where(which == d, dl[d], 0.0) for d in range(4))
        dtab[...] = jnp.exp(dot(table(rows[:, :head_count]), hot[...]))
        for u in range(2):
            to_core(u).wait_recv()
            at = quarter(u, core)
            theirs = jnp.where(core == 1, dtab[0:1, at], 1.0)
            ours = jnp.where(core == 1, 1.0, dtab[1:2, at])
            tc[u] = (theirs * s1[u].astype(F32) + ours * tot[:, at].astype(F32)).astype(BF16)
        to_row().start()

    def pass_state():
        to_row().wait_recv()

        @pl.when(has_z)
        def _():
            to_next().wait_recv()

        at = quarter(row, core)
        near = dtab[0:1, at] * dtab[1:2, at]
        far = dtab[2:3, at] * dtab[3:4, at]
        entry = ein[...]
        ours, theirs = tc[row].astype(F32), s2[...].astype(F32)
        quad = jnp.where(row == 1, near, 1.0) * theirs + jnp.where(row == 1, 1.0, far) * ours

        @pl.when(has_next)
        def _():
            eout[...] = near * far * entry + quad
            to_next().start()

        s4out[...] = jnp.where(row == 0, near * entry + ours, entry).astype(BF16)
        back_row().start()
        ec[row] = jnp.where(row == 0, entry, far * entry + theirs).astype(BF16)

    def pass_core():
        back_row().wait_recv()
        for u in range(2):
            at = quarter(u, core)
            entry = ec[u].astype(F32)
            later = jnp.where(core == 0, dtab[0:1, at], dtab[1:2, at]) * entry
            later = later + jnp.where(core == 0, tot[:, at], s1[u]).astype(F32)
            s5out[u] = jnp.where(core == 0, later, entry).astype(BF16)
            back_core(u).start()
            carried[:, at] = jnp.where(core == 0, entry, later).astype(BF16)

    turn = jnp.minimum(3 + 2 * z, 9)
    ready = turn + 3

    def step(j, carry):
        @pl.when(j < heads)
        def _():
            @pl.when(has_z)
            def _():
                arrived(Z, j)

                @pl.when(row == 1)
                def _():
                    whole(Y, j, Z).start()

                @pl.when(core == 1)
                def _():
                    whole(B, j, Z).start()

        @pl.when(j == 1)
        def _():
            chip_totals()

        @pl.when(j == turn)
        def _():
            pass_state()

        @pl.when(j == turn + 2)
        def _():
            pass_core()

        @pl.when(j < heads)
        def _():
            @pl.when(has_next)
            def _():
                sent(Z, j)

            @pl.when(j + 2 < heads)
            def _():
                offer(j + 2)

        @pl.when(j == 0)
        def _():
            lax.fori_loop(0, pairs, local_state, 0)
            for u in range(2):
                to_core(u).start()
            for one in loads[4:]:
                one.wait()

        @pl.when(j >= 2)
        def _():
            @pl.when(has_y)
            def _():
                arrived(A, j - 2)

            second_part(j - 2)

        @pl.when((j >= 1) & (j <= heads))
        def _():
            @pl.when(has_b)
            def _():
                arrived(B, j - 1)

            first_part(j - 1)

        half = (pairs + 7) // 8

        @pl.when((j >= 1) & (j <= 8))
        def _():
            lax.fori_loop((j - 1) * half, jnp.minimum(j * half, pairs), intra, 0)

        fourth = (pairs + 3) // 4

        @pl.when((j >= ready) & (j < ready + 4))
        def _():
            @pl.when(j == ready)
            def _():
                for u in range(2):
                    back_core(u).wait_recv()

            first = (j - ready) * fourth
            lax.fori_loop(first, jnp.minimum(first + fourth, pairs), finish, 0)

        @pl.when((j >= 1) & (j <= heads) & has_y)
        def _():
            arrived(Y, j - 1)
            whole(A, j - 1, Y).start()

        return carry

    lax.fori_loop(0, heads + 2, step, 0)

    for d in range(1, 4):
        own_dl(d).wait_send()
    for u in range(2):
        to_core(u).wait_send()
        back_core(u).wait_send()
    to_row().wait_send()
    back_row().wait_send()

    @pl.when(has_next)
    def _():
        to_next().wait_send()

    def drain(h, carry):
        @pl.when(has_z | (row == 0))
        def _():
            sent(Y, h)

        @pl.when(has_y)
        def _():
            sent(A, h)

        @pl.when(has_z | (core == 0))
        def _():
            sent(B, h)

        return carry

    lax.fori_loop(0, heads, drain, 0)


def on_device(queries, keys, values, ssd_input, bmat, cmat, expo, rate, skip):
    length, total_cols = queries.shape
    size = lax.axis_size("seq")
    head_count = rate.shape[0]
    x_cols = ssd_input.shape[1]
    state = cmat.shape[1]
    heads = total_cols // E
    blocks = length // Q
    group = x_cols // 4
    vmem = pl.BlockSpec(memory_space=pltpu.VMEM)
    anywhere = pl.BlockSpec(memory_space=pl.ANY)
    dma = pltpu.SemaphoreType.DMA
    inputs = (queries, keys, values, ssd_input, bmat, cmat, expo.T)
    big = [pltpu.VMEM(a.shape, a.dtype) for a in inputs]
    return pl.pallas_call(
        functools.partial(kernel, size),
        in_specs=[anywhere] * 7 + [vmem] * 2,
        out_specs=(vmem, vmem),
        out_shape=(
            jax.ShapeDtypeStruct(queries.shape, BF16),
            jax.ShapeDtypeStruct(ssd_input.shape, BF16),
        ),
        scratch_shapes=[
            *big,
            pltpu.VMEM((4, heads, 2, length, E), BF16),
            pltpu.VMEM((LANES, x_cols), BF16),
            pltpu.VMEM((length, LANES), BF16),
            pltpu.VMEM((head_count, length), F32),
            pltpu.VMEM((state, length), BF16),
            pltpu.VMEM((blocks, Q, Q), F32),
            pltpu.VMEM((8, x_cols), F32),
            pltpu.VMEM((8, x_cols), F32),
            pltpu.VMEM((4, 8, LANES), F32),
            pltpu.VMEM((8, x_cols), F32),
            pltpu.VMEM((blocks, state, x_cols), F32),
            pltpu.VMEM((state, x_cols), BF16),
            pltpu.VMEM((2, state, group), BF16),
            pltpu.VMEM((2, state, group), BF16),
            pltpu.VMEM((state, group), BF16),
            pltpu.VMEM((state, group), F32),
            pltpu.VMEM((state, group), F32),
            pltpu.VMEM((state, group), BF16),
            pltpu.VMEM((2, state, group), BF16),
            pltpu.VMEM((2, state, group), BF16),
            pltpu.VMEM((state, x_cols), BF16),
            pltpu.VMEM((length, x_cols), F32),
            pltpu.VMEM((length, E), F32),
            pltpu.VMEM((2, length, E), F32),
            dma((7,)),
            dma((4, heads)),
            dma((4, heads)),
            dma((4,)),
            dma((4,)),
            dma((2,)),
            dma((2,)),
            dma((2,)),
            dma((2,)),
            dma((3,)),
            dma((3,)),
        ],
        compiler_params=pltpu.CompilerParams(
            collective_id=0, has_side_effects=True, vmem_limit_bytes=60 << 20
        ),
        name="attention_and_recurrence",
    )(*inputs, rate[None, :], skip[None, :])


def solution(mesh):
    split_rows = P(("groups", "seq"), None)
    return jax.shard_map(
        on_device,
        mesh=mesh,
        in_specs=(split_rows,) * 7 + (P(), P()),
        out_specs=(split_rows, split_rows),
        check_vma=False,
    )
```

time: 189 us -> 129 us (0.68)
  Pallas kernels: 173 us -> 123 us
  local copies, waits for them, and re-layouts: 11.2 us -> 4.63 us
  other arithmetic: 2.98 us -> 0 us
    pallas_call x1, Pallas kernels: 173 us -> 123 us  [on_device(): pl.pallas_call(functools.partial(kernel, size), in_specs=[anywhere] * 7 +...]
    unnamed x7 -> x4, local copies, waits for them, and re-layouts: 6.29 us -> 4.63 us
where the time goes in v1:
time: 129 us; the launch traced here: 128 us
  Pallas kernels  123 us (95%)
  local copies, waits for them, and re-layouts  4.63 us (4%)
    pallas_call x1, Pallas kernels, on_device(): pl.pallas_call(functools.partial(kernel, size), in_specs=[anywhere] * 7 +...  123 us
    unnamed x4, local copies, waits for them, and re-layouts  4.63 us

profile of v1, /device:TPU:9, one launch (start us, length us, event | category | flops | bytes accessed | tf_op | source)
XLA Modules:
  0.0 128.1 jit_solution(10166209692561137168)
XLA Ops:
  0.6 122.9 %attention_and_recurrence.1 = (bf16[512,2048]{1,0:T(8,128)(2,1)}, bf16[512,2048]{1,0:T(8,128)(2,1)}) custom-call(bf16[512,2048]{1,0:T(8,128)(2,1)} %q_in.1, bf16[512,2048]{1,0:T(8,128)(2,1)} %k_in.1, bf16[512,2048]{1,0:T(8,128)(2,1)} %v_in.1, bf16[512,2048]{1,0:T(8,128)(2,1)} %x_in.1, bf16[512,128]{1,0:T(8,128)(2,1)} %b_in.1, bf16[512,128]{1,0:T(8,128)(2,1)} %c_in.1, ...), custom_call_target="tpu_custom_call" | custom-call | tf_op jit(solution)/shard_map/attention_and_recurrence/pallas_call | solution.py:539
  123.5 0.0 copy-start
  123.5 3.3 %copy.13 = bf16[512,2048]{1,0:T(8,128)(2,1)} copy(bf16[512,2048]{1,0:T(8,128)(2,1)} %get-tuple-element.4) | data formatting | bytes 4194304
  126.8 0.0 copy-done
  126.8 1.3 %copy.14 = bf16[512,2048]{1,0:T(8,128)(2,1)} copy(bf16[512,2048]{1,0:T(8,128)(2,1)S(1)} %copy-done) | data formatting | bytes 4194304
Async XLA Ops:
  123.5 3.3 %copy-start = (bf16[512,2048]{1,0:T(8,128)(2,1)S(1)}, bf16[512,2048]{1,0:T(8,128)(2,1)}, u32[]{:S(2)}) copy-start(bf16[512,2048]{1,0:T(8,128)(2,1)} %get-tuple-element.5) | copy-start | bytes 6291460

commit v2 on v1

--- a/solution.py
+++ b/solution.py
@@ -79,8 +79,8 @@
 
 
 def kernel(
-    size, q_in, k_in, v_in, x_in, b_in, c_in, expo_in, rate_ref, skip_ref, attn_ref, rec_ref,
-    q_ref, k_ref, v_ref, x_ref, b_ref, c_ref, expo_ref, held, hot, t3, cumt, bt, cross, dec, skx,
+    size, q_in, k_in, v_in, x_in, b_in, c_in, expo_in, rate_in, skip_in, attn_ref, rec_ref,
+    q_ref, k_ref, v_ref, x_ref, b_ref, c_ref, expo_ref, rate_ref, skip_ref, held, hot, t3, cumt, bt, cross, dec, skx,
     dl, dtab, local, tot, s1, tc, s2, ein, eout, s4out, ec, s5out, carried, mixed, acc_ref, ml_ref,
     load, send, recv, dl_send, dl_recv, s1_send, s1_recv, s5_send, s5_recv, one_send, one_recv,
 ):
@@ -120,11 +120,11 @@
         )
 
     inputs = (
-        (expo_in, expo_ref), (b_in, b_ref), (c_in, c_ref), (x_in, x_ref), (q_in, q_ref),
-        (k_in, k_ref), (v_in, v_ref),
+        (rate_in, rate_ref), (expo_in, expo_ref), (skip_in, skip_ref), (b_in, b_ref), (c_in, c_ref),
+        (x_in, x_ref), (q_in, q_ref), (k_in, k_ref), (v_in, v_ref),
     )
     loads = [pltpu.make_async_copy(a, b, load.at[i]) for i, (a, b) in enumerate(inputs)]
-    for one in loads[:4]:
+    for one in loads[:6]:
         one.start()
 
     barrier = pltpu.get_barrier_semaphore()
@@ -176,7 +176,7 @@
 
     offer(0)
     offer(1)
-    for one in loads[4:]:
+    for one in loads[6:]:
         one.start()
 
     def own_dl(d):
@@ -218,6 +218,7 @@
     low = iota((Q, Q), 1) <= iota((Q, Q), 0)
     upto = jnp.where(iota((Q, Q), 0) <= iota((Q, Q), 1), 1.0, 0.0).astype(BF16)
     loads[0].wait()
+    loads[1].wait()
     rates = wide(rate_ref[...])[0:1, :]
     rates = jnp.broadcast_to(rates, (LANES, LANES)).T[0:head_count, 0:1]
     dlog = None
@@ -234,14 +235,15 @@
     dl[0] = jnp.broadcast_to(wide(dlog), dl.shape[1:])
     for d in range(1, 4):
         own_dl(d).start()
+    loads[2].wait()
     skx[...] = jnp.broadcast_to(dot(table(skip_ref[...]), hot[...]), skx.shape)
-    loads[1].wait()
-    loads[2].wait()
+    loads[3].wait()
+    loads[4].wait()
     bt[...] = b_ref[...].astype(F32).T.astype(BF16)
     for b in range(blocks):
         rs = slice(b * Q, (b + 1) * Q)
         cross[b] = jnp.where(low, dot_t(c_ref[rs, :], b_ref[rs, :]), 0.0)
-    loads[3].wait()
+    loads[5].wait()
 
     lane = iota((1, LANES), 1)
 
@@ -443,10 +445,10 @@
 
         @pl.when(j == 0)
         def _():
-            lax.fori_loop(0, pairs, local_state, 0)
+            lax.fori_loop(0, pairs, local_state, 0, unroll=4)
             for u in range(2):
                 to_core(u).start()
-            for one in loads[4:]:
+            for one in loads[6:]:
                 one.wait()
 
         @pl.when(j >= 2)
@@ -457,6 +459,11 @@
 
             second_part(j - 2)
 
+        @pl.when((j >= 1) & (j <= heads) & has_y)
+        def _():
+            arrived(Y, j - 1)
+            whole(A, j - 1, Y).start()
+
         @pl.when((j >= 1) & (j <= heads))
         def _():
             @pl.when(has_b)
@@ -465,13 +472,12 @@
 
             first_part(j - 1)
 
-        half = (pairs + 7) // 8
-
-        @pl.when((j >= 1) & (j <= 8))
-        def _():
-            lax.fori_loop((j - 1) * half, jnp.minimum(j * half, pairs), intra, 0)
-
-        fourth = (pairs + 3) // 4
+        @pl.when((j >= 1) & (j <= pairs // 2))
+        def _():
+            for n in range(2):
+                intra(2 * (j - 1) + n, 0)
+
+        fourth = pairs // 4
 
         @pl.when((j >= ready) & (j < ready + 4))
         def _():
@@ -480,13 +486,8 @@
                 for u in range(2):
                     back_core(u).wait_recv()
 
-            first = (j - ready) * fourth
-            lax.fori_loop(first, jnp.minimum(first + fourth, pairs), finish, 0)
-
-        @pl.when((j >= 1) & (j <= heads) & has_y)
-        def _():
-            arrived(Y, j - 1)
-            whole(A, j - 1, Y).start()
+            for n in range(fourth):
+                finish((j - ready) * fourth + n, 0)
 
         return carry
 
@@ -532,13 +533,14 @@
     blocks = length // Q
     group = x_cols // 4
     vmem = pl.BlockSpec(memory_space=pltpu.VMEM)
-    anywhere = pl.BlockSpec(memory_space=pl.ANY)
     dma = pltpu.SemaphoreType.DMA
-    inputs = (queries, keys, values, ssd_input, bmat, cmat, expo.T)
+    inputs = (
+        queries, keys, values, ssd_input, bmat, cmat, expo.T, rate[None, :], skip[None, :]
+    )
     big = [pltpu.VMEM(a.shape, a.dtype) for a in inputs]
     return pl.pallas_call(
         functools.partial(kernel, size),
-        in_specs=[anywhere] * 7 + [vmem] * 2,
+        in_specs=[pl.BlockSpec(memory_space=pltpu.HBM)] * len(inputs),
         out_specs=(vmem, vmem),
         out_shape=(
             jax.ShapeDtypeStruct(queries.shape, BF16),
@@ -570,7 +572,7 @@
             pltpu.VMEM((length, x_cols), F32),
             pltpu.VMEM((length, E), F32),
             pltpu.VMEM((2, length, E), F32),
-            dma((7,)),
+            dma((9,)),
             dma((4, heads)),
             dma((4, heads)),
             dma((4,)),
@@ -583,10 +585,10 @@
             dma((3,)),
         ],
         compiler_params=pltpu.CompilerParams(
-            collective_id=0, has_side_effects=True, vmem_limit_bytes=60 << 20
+            collective_id=0, has_side_effects=True, vmem_limit_bytes=48 << 20
         ),
         name="attention_and_recurrence",
-    )(*inputs, rate[None, :], skip[None, :])
+    )(*(pltpu.with_memory_space_constraint(a, pltpu.HBM) for a in inputs))
 
 
 def solution(mesh):

time: 129 us -> 117 us (0.907)
  Pallas kernels: 123 us -> 113 us
  local copies, waits for them, and re-layouts: 4.63 us -> 2.64 us
    pallas_call x1, Pallas kernels: 123 us -> 113 us  [on_device(): pl.pallas_call(functools.partial(kernel, size), in_specs=[pl.BlockSpec(me...]
    unnamed x4 -> x2, local copies, waits for them, and re-layouts: 4.63 us -> 2.64 us
where the time goes in v2:
time: 117 us; the launch traced here: 116 us
  Pallas kernels  113 us (97%)
  local copies, waits for them, and re-layouts  2.64 us (2%)
    pallas_call x1, Pallas kernels, on_device(): pl.pallas_call(functools.partial(kernel, size), in_specs=[pl.BlockSpec(me...  113 us
    unnamed x2, local copies, waits for them, and re-layouts  2.64 us

profile of v2, /device:TPU:9, one launch (start us, length us, event | category | flops | bytes accessed | tf_op | source)
XLA Modules:
  0.0 116.3 jit_solution(12388944751272069071)
XLA Ops:
  0.6 113.0 %attention_and_recurrence.1 = (bf16[512,2048]{1,0:T(8,128)(2,1)S(1)}, bf16[512,2048]{1,0:T(8,128)(2,1)S(1)}) custom-call(bf16[512,2048]{1,0:T(8,128)(2,1)} %q_in.1, bf16[512,2048]{1,0:T(8,128)(2,1)} %k_in.1, bf16[512,2048]{1,0:T(8,128)(2,1)} %v_in.1, bf16[512,2048]{1,0:T(8,128)(2,1)} %x_in.1, bf16[512,128]{1,0:T(8,128)(2,1)} %b_in.1, bf16[512,128]{1,0:T(8,128)(2,1)} %c_in.1, ...), custom_call_target="tpu_custom_call" | custom-call | tf_op jit(solution)/shard_map/attention_and_recurrence/pallas_call | solution.py:541
  113.6 1.3 %copy.13 = bf16[512,2048]{1,0:T(8,128)(2,1)} copy(bf16[512,2048]{1,0:T(8,128)(2,1)S(1)} %get-tuple-element.4) | data formatting | bytes 4194304
  115.0 1.3 %copy.14 = bf16[512,2048]{1,0:T(8,128)(2,1)} copy(bf16[512,2048]{1,0:T(8,128)(2,1)S(1)} %get-tuple-element.5) | data formatting | bytes 4194304

commit v3 on v2

--- a/solution.py
+++ b/solution.py
@@ -82,7 +82,7 @@
     size, q_in, k_in, v_in, x_in, b_in, c_in, expo_in, rate_in, skip_in, attn_ref, rec_ref,
     q_ref, k_ref, v_ref, x_ref, b_ref, c_ref, expo_ref, rate_ref, skip_ref, held, hot, t3, cumt, bt, cross, dec, skx,
     dl, dtab, local, tot, s1, tc, s2, ein, eout, s4out, ec, s5out, carried, mixed, acc_ref, ml_ref,
-    load, send, recv, dl_send, dl_recv, s1_send, s1_recv, s5_send, s5_recv, one_send, one_recv,
+    load, z_send, z_recv, edge_recv, side_send, side_recv, dl_send, dl_recv, s1_send, s1_recv, s5_send, s5_recv, one_send, one_recv,
 ):
     nz = size // 4
     here = lax.axis_index("seq")
@@ -143,39 +143,92 @@
 
     target = {Z: beyond(1), Y: beside(2), A: beside(1), B: beside(1)}
 
-    def send_own(kind, h):
-        for part, ref in ((0, k_in), (1, v_in)):
-            copy(
-                ref.at[:, lanes_of(h)], held.at[kind, h, part], send.at[kind, h], recv.at[kind, h],
-                target[kind],
-            ).start()
-
-    def whole(kind, h, source):
+    def side(kind, h, source):
         return copy(
-            held.at[source, h], held.at[kind, h], send.at[kind, h], recv.at[kind, h], target[kind]
+            held.at[source, h], held.at[kind, h], side_send.at[kind - 1], side_recv.at[kind - 1, h],
+            target[kind],
         )
 
     def arrived(kind, h):
-        whole(kind, h, kind).wait_recv()
-
-    def sent(kind, h):
-        whole(kind, h, kind).wait_send()
-
-    def offer(h):
+        side(kind, h, kind).wait_recv()
+
+    def all_sent(kind):
+        copy(
+            held.at[kind], held.at[kind], side_send.at[kind - 1], side_recv.at[kind - 1, 0],
+            target[kind],
+        ).wait_send()
+
+    piece = length // 4
+    halves = [(part, slice(0, length)) for part in range(2)]
+    pieces = [(part, slice(i * piece, (i + 1) * piece)) for part in range(2) for i in range(4)]
+
+    def z_copy(h, n, cut, arrival):
+        part, rows = cut[n]
+        return copy(
+            (k_in, v_in)[part].at[rows, lanes_of(h)], held.at[Z, h, part, rows], z_send.at[h],
+            arrival(n), target[Z],
+        )
+
+    def z_relay(h, n, cut, kind):
+        part, rows = cut[n]
+        return copy(
+            held.at[Z, h, part, rows], held.at[kind, h, part, rows], side_send.at[kind - 1],
+            side_recv.at[kind - 1, h], target[kind],
+        )
+
+    def first_sems(n):
+        return edge_recv.at[0, n]
+
+    def last_sems(n):
+        return edge_recv.at[1, n]
+
+    def z_arrived(h, n, cut, arrival):
+        @pl.when(has_z)
+        def _():
+            z_copy(h, n, cut, arrival).wait_recv()
+
+            @pl.when(row == 1)
+            def _():
+                z_relay(h, n, cut, Y).start()
+
+            @pl.when(core == 1)
+            def _():
+                z_relay(h, n, cut, B).start()
+
+    def z_sent(h):
+        copy(
+            held.at[Z, h], held.at[Z, h], z_send.at[h], z_recv.at[h, 0], target[Z]
+        ).wait_send()
+
+    def z_offer(h, cut, arrival):
         @pl.when(has_next)
         def _():
-            send_own(Z, h)
+            for n in range(len(cut)):
+                z_copy(h, n, cut, arrival).start()
+
+    def side_offer(h):
+        def send_own(kind):
+            for part, ref in ((0, k_in), (1, v_in)):
+                copy(
+                    ref.at[:, lanes_of(h)], held.at[kind, h, part], side_send.at[kind - 1],
+                    side_recv.at[kind - 1, h], target[kind],
+                ).start()
 
         @pl.when(row == 0)
         def _():
-            send_own(Y, h)
+            send_own(Y)
 
         @pl.when(core == 0)
         def _():
-            send_own(B, h)
-
-    offer(0)
-    offer(1)
+            send_own(B)
+
+    def z_sems(h):
+        return lambda n: z_recv.at[h, n]
+
+    z_offer(0, pieces, first_sems)
+    side_offer(0)
+    z_offer(1, halves, z_sems(1))
+    side_offer(1)
     for one in loads[6:]:
         one.start()
 
@@ -310,32 +363,40 @@
 
     bias = {Z: off(has_z), Y: off(has_y), A: off(has_y), B: off(has_b)}
 
+    def keep(rows, m, l, acc):
+        acc_ref[rows, :] = acc
+        ml_ref[0, rows, :] = jnp.broadcast_to(m, acc.shape)
+        ml_ref[1, rows, :] = jnp.broadcast_to(l, acc.shape)
+
+    def more(h, kind, rows):
+        return flash(
+            q_ref[rows, lanes_of(h)], [(held[kind, h, 0], held[kind, h, 1], bias[kind], None)],
+            ml_ref[0, rows, 0:1], ml_ref[1, rows, 0:1], acc_ref[rows, :],
+        )
+
+    query_rows = [slice(r, r + tq) for r in range(0, length, tq)]
+
     def first_part(h):
         hs = lanes_of(h)
-        for r in range(0, length, tq):
-            rows = slice(r, r + tq)
+        for rows in query_rows:
             tiles = [(k_ref[rows, hs], v_ref[rows, hs], None, "low")]
-            if r > 0:
-                tiles.append((k_ref[0:r, hs], v_ref[0:r, hs], None, None))
+            if rows.start > 0:
+                tiles.append((k_ref[0 : rows.start, hs], v_ref[0 : rows.start, hs], None, None))
             tiles.append((held[Z, h, 0, rows, :], held[Z, h, 1, rows, :], bias[Z], "up"))
-            if r + tq < length:
-                past = slice(r + tq, length)
+            if rows.stop < length:
+                past = slice(rows.stop, length)
                 tiles.append((held[Z, h, 0, past, :], held[Z, h, 1, past, :], bias[Z], None))
             tiles.append((held[B, h, 0], held[B, h, 1], bias[B], None))
-            m, l, acc = flash(q_ref[rows, hs], tiles, None, None, None)
-            acc_ref[rows, :] = acc
-            ml_ref[0, rows, :] = jnp.broadcast_to(m, acc.shape)
-            ml_ref[1, rows, :] = jnp.broadcast_to(l, acc.shape)
+            keep(rows, *flash(q_ref[rows, hs], tiles, None, None, None))
 
     def second_part(h):
-        hs = lanes_of(h)
-        for r in range(0, length, tq):
-            rows = slice(r, r + tq)
-            tiles = [(held[n, h, 0], held[n, h, 1], bias[n], None) for n in (Y, A)]
-            m, l, acc = flash(
-                q_ref[rows, hs], tiles, ml_ref[0, rows, 0:1], ml_ref[1, rows, 0:1], acc_ref[rows, :]
-            )
-            attn_ref[rows, hs] = (acc / l).astype(attn_ref.dtype)
+        for rows in query_rows:
+            keep(rows, *more(h, Y, rows))
+
+    def third_part(h):
+        for rows in query_rows:
+            m, l, acc = more(h, A, rows)
+            attn_ref[rows, lanes_of(h)] = (acc / l).astype(attn_ref.dtype)
 
     @pl.when(z == 0)
     def _():
@@ -355,12 +416,17 @@
 
         lax.fori_loop(0, heads, clear, 0)
 
+    def decays(*which):
+        for d in which:
+            if d:
+                own_dl(d).wait_recv()
+        line = iota((8, LANES), 0)
+        rows = sum(jnp.where(line == i, dl[d], 0.0) for i, d in enumerate(which))
+        spread_out = jnp.exp(dot(table(rows[:, :head_count]), hot[...]))
+        dtab[which[0] : which[0] + 2, :] = spread_out[0:2, :]
+
     def chip_totals():
-        for d in range(1, 4):
-            own_dl(d).wait_recv()
-        which = iota((8, LANES), 0)
-        rows = sum(jnp.where(which == d, dl[d], 0.0) for d in range(4))
-        dtab[...] = jnp.exp(dot(table(rows[:, :head_count]), hot[...]))
+        decays(0, 1)
         for u in range(2):
             to_core(u).wait_recv()
             at = quarter(u, core)
@@ -370,6 +436,7 @@
         to_row().start()
 
     def pass_state():
+        decays(2, 3)
         to_row().wait_recv()
 
         @pl.when(has_z)
@@ -379,13 +446,13 @@
         at = quarter(row, core)
         near = dtab[0:1, at] * dtab[1:2, at]
         far = dtab[2:3, at] * dtab[3:4, at]
-        entry = ein[...]
+        entry = ein[...].astype(F32)
         ours, theirs = tc[row].astype(F32), s2[...].astype(F32)
         quad = jnp.where(row == 1, near, 1.0) * theirs + jnp.where(row == 1, 1.0, far) * ours
 
         @pl.when(has_next)
         def _():
-            eout[...] = near * far * entry + quad
+            eout[...] = (near * far * entry + quad).astype(BF16)
             to_next().start()
 
         s4out[...] = jnp.where(row == 0, near * entry + ours, entry).astype(BF16)
@@ -403,81 +470,86 @@
             back_core(u).start()
             carried[:, at] = jnp.where(core == 0, entry, later).astype(BF16)
 
-    turn = jnp.minimum(3 + 2 * z, 9)
-    ready = turn + 3
+    turn = jnp.minimum(2 + 2 * z, 8)
+    ready = turn + 2
+    fourth = pairs // 4
+
+    lax.fori_loop(0, pairs // 2, local_state, 0, unroll=4)
+    z_arrived(0, 0, pieces, first_sems)
+    lax.fori_loop(pairs // 2, pairs, local_state, 0, unroll=4)
+    for u in range(2):
+        to_core(u).start()
+    for n in range(1, len(pieces)):
+        z_arrived(0, n, pieces, first_sems)
+    for one in loads[6:]:
+        one.wait()
 
     def step(j, carry):
-        @pl.when(j < heads)
-        def _():
-            @pl.when(has_z)
-            def _():
-                arrived(Z, j)
-
-                @pl.when(row == 1)
-                def _():
-                    whole(Y, j, Z).start()
-
-                @pl.when(core == 1)
-                def _():
-                    whole(B, j, Z).start()
-
-        @pl.when(j == 1)
+        @pl.when(j == turn)
+        def _():
+            pass_state()
+
+        @pl.when((j < heads - 1) & (j >= 1))
+        def _():
+            for n in range(2):
+                z_arrived(j, n, halves, z_sems(j))
+
+        @pl.when(j == heads - 1)
+        def _():
+            for n in range(len(pieces)):
+                z_arrived(heads - 1, n, pieces, last_sems)
+
+        @pl.when(j == 0)
         def _():
             chip_totals()
 
-        @pl.when(j == turn)
-        def _():
-            pass_state()
-
-        @pl.when(j == turn + 2)
+        @pl.when((j < heads) & has_next)
+        def _():
+            z_sent(j)
+
+        @pl.when(j + 2 < heads)
+        def _():
+            @pl.when(j + 3 < heads)
+            def _():
+                z_offer(j + 2, halves, z_sems(j + 2))
+
+            @pl.when(j + 3 == heads)
+            def _():
+                z_offer(heads - 1, pieces, last_sems)
+
+            side_offer(j + 2)
+
+        @pl.when(j >= 2)
+        def _():
+            @pl.when(has_y)
+            def _():
+                arrived(A, j - 2)
+
+            third_part(j - 2)
+
+        @pl.when((j >= 1) & (j <= heads))
+        def _():
+            @pl.when(has_b)
+            def _():
+                arrived(B, j - 1)
+
+            first_part(j - 1)
+
+            @pl.when(has_y)
+            def _():
+                arrived(Y, j - 1)
+                side(A, j - 1, Y).start()
+
+            second_part(j - 1)
+
+        @pl.when(j == turn + 1)
         def _():
             pass_core()
 
-        @pl.when(j < heads)
-        def _():
-            @pl.when(has_next)
-            def _():
-                sent(Z, j)
-
-            @pl.when(j + 2 < heads)
-            def _():
-                offer(j + 2)
-
-        @pl.when(j == 0)
-        def _():
-            lax.fori_loop(0, pairs, local_state, 0, unroll=4)
-            for u in range(2):
-                to_core(u).start()
-            for one in loads[6:]:
-                one.wait()
-
-        @pl.when(j >= 2)
-        def _():
-            @pl.when(has_y)
-            def _():
-                arrived(A, j - 2)
-
-            second_part(j - 2)
-
-        @pl.when((j >= 1) & (j <= heads) & has_y)
-        def _():
-            arrived(Y, j - 1)
-            whole(A, j - 1, Y).start()
-
-        @pl.when((j >= 1) & (j <= heads))
-        def _():
-            @pl.when(has_b)
-            def _():
-                arrived(B, j - 1)
-
-            first_part(j - 1)
-
-        @pl.when((j >= 1) & (j <= pairs // 2))
+        @pl.when(j < pairs // 2)
         def _():
             for n in range(2):
-                intra(2 * (j - 1) + n, 0)
-
-        fourth = pairs // 4
+                intra(2 * j + n, 0)
 
         @pl.when((j >= ready) & (j < ready + 4))
         def _():
@@ -505,22 +577,17 @@
     def _():
         to_next().wait_send()
 
-    def drain(h, carry):
-        @pl.when(has_z | (row == 0))
-        def _():
-            sent(Y, h)
-
-        @pl.when(has_y)
-        def _():
-            sent(A, h)
-
-        @pl.when(has_z | (core == 0))
-        def _():
-            sent(B, h)
-
-        return carry
-
-    lax.fori_loop(0, heads, drain, 0)
+    @pl.when(has_z | (row == 0))
+    def _():
+        all_sent(Y)
+
+    @pl.when(has_y)
+    def _():
+        all_sent(A)
+
+    @pl.when(has_z | (core == 0))
+    def _():
+        all_sent(B)
 
 
 def on_device(queries, keys, values, ssd_input, bmat, cmat, expo, rate, skip):
@@ -563,8 +630,8 @@
             pltpu.VMEM((2, state, group), BF16),
             pltpu.VMEM((2, state, group), BF16),
             pltpu.VMEM((state, group), BF16),
-            pltpu.VMEM((state, group), F32),
-            pltpu.VMEM((state, group), F32),
+            pltpu.VMEM((state, group), BF16),
+            pltpu.VMEM((state, group), BF16),
             pltpu.VMEM((state, group), BF16),
             pltpu.VMEM((2, state, group), BF16),
             pltpu.VMEM((2, state, group), BF16),
@@ -573,8 +640,11 @@
             pltpu.VMEM((length, E), F32),
             pltpu.VMEM((2, length, E), F32),
             dma((9,)),
-            dma((4, heads)),
-            dma((4, heads)),
+            dma((heads,)),
+            dma((heads, 2)),
+            dma((2, 8)),
+            dma((3,)),
+            dma((3, heads)),
             dma((4,)),
             dma((4,)),
             dma((2,)),

time: 117 us -> 113 us (0.966)
  Pallas kernels: 113 us -> 109 us
    pallas_call x1, Pallas kernels: 113 us -> 109 us  [on_device(): pl.pallas_call(functools.partial(kernel, size), in_specs=[pl.BlockSpec(me...]
where the time goes in v3:
time: 113 us; the launch traced here: 112 us
  Pallas kernels  109 us (96%)
  local copies, waits for them, and re-layouts  2.64 us (2%)
    pallas_call x1, Pallas kernels, on_device(): pl.pallas_call(functools.partial(kernel, size), in_specs=[pl.BlockSpec(me...  109 us
    unnamed x2, local copies, waits for them, and re-layouts  2.64 us

profile of v3, /device:TPU:9, one launch (start us, length us, event | category | flops | bytes accessed | tf_op | source)
XLA Modules:
  0.0 112.4 jit_solution(13611800346760457110)
XLA Ops:
  0.6 109.1 %attention_and_recurrence.1 = (bf16[512,2048]{1,0:T(8,128)(2,1)S(1)}, bf16[512,2048]{1,0:T(8,128)(2,1)S(1)}) custom-call(bf16[512,2048]{1,0:T(8,128)(2,1)} %q_in.1, bf16[512,2048]{1,0:T(8,128)(2,1)} %k_in.1, bf16[512,2048]{1,0:T(8,128)(2,1)} %v_in.1, bf16[512,2048]{1,0:T(8,128)(2,1)} %x_in.1, bf16[512,128]{1,0:T(8,128)(2,1)} %b_in.1, bf16[512,128]{1,0:T(8,128)(2,1)} %c_in.1, ...), custom_call_target="tpu_custom_call" | custom-call | tf_op jit(solution)/shard_map/attention_and_recurrence/pallas_call | solution.py:608
  109.7 1.3 %copy.13 = bf16[512,2048]{1,0:T(8,128)(2,1)} copy(bf16[512,2048]{1,0:T(8,128)(2,1)S(1)} %get-tuple-element.4) | data formatting | bytes 4194304
  111.1 1.3 %copy.14 = bf16[512,2048]{1,0:T(8,128)(2,1)} copy(bf16[512,2048]{1,0:T(8,128)(2,1)S(1)} %get-tuple-element.5) | data formatting | bytes 4194304

commit v4 on v3

--- a/solution.py
+++ b/solution.py
@@ -55,18 +55,18 @@
 def flash(q, tiles, m, l, acc):
     tq = q.shape[0]
     scale = LOG2E / math.sqrt(E)
-    for k, v, bias, mask in tiles:
+    for k, v, mask in tiles:
         s = dot_t(q, k) * scale
         if mask is not None:
             row, col = iota((tq, tq), 0), iota((tq, tq), 1)
             s = jnp.where(col <= row if mask == "low" else col > row, s, NEG)
-        peak = jnp.max(s, axis=1, keepdims=True)
-        if bias is not None:
-            peak = peak + bias
+        groups = s.shape[1] // LANES
+        peak = jnp.broadcast_to(jnp.max(s, axis=1, keepdims=True), (tq, LANES))
         m_new = peak if m is None else jnp.maximum(m, peak)
-        shift = m_new if bias is None else m_new - bias
-        p = jnp.exp2(s - shift)
-        total = jnp.sum(p, axis=1, keepdims=True)
+        p = jnp.exp2(s - jnp.concatenate([m_new] * groups, axis=1))
+        total = p[:, 0:LANES]
+        for g in range(1, groups):
+            total = total + p[:, g * LANES : (g + 1) * LANES]
         part = dot(p.astype(BF16), v)
         if m is None:
             l, acc = total, part
@@ -78,11 +78,18 @@
     return m, l, acc
 
 
+def whole_sum(l):
+    return jnp.sum(l, axis=1, keepdims=True)
+
+
 def kernel(
     size, q_in, k_in, v_in, x_in, b_in, c_in, expo_in, rate_in, skip_in, attn_ref, rec_ref,
-    q_ref, k_ref, v_ref, x_ref, b_ref, c_ref, expo_ref, rate_ref, skip_ref, held, hot, t3, cumt, bt, cross, dec, skx,
-    dl, dtab, local, tot, s1, tc, s2, ein, eout, s4out, ec, s5out, carried, mixed, acc_ref, ml_ref,
-    load, z_send, z_recv, edge_recv, side_send, side_recv, dl_send, dl_recv, s1_send, s1_recv, s5_send, s5_recv, one_send, one_recv,
+    q_ref, k_ref, v_ref, x_ref, b_ref, c_ref, expo_ref, rate_ref, skip_ref, held, hot, t3, cumt, bt,
+    cross, dec, skx, dl, dtab, local, tot, s1, tc, s2, ein, eout, s4out, ec, s5out, carried, mixed,
+    acc_ref, ml_ref, q_now, up_q, up_o, up_s, down_o, down_s, row_q, row_o, row_s, back_o, back_s,
+    load, z_send, z_recv, last_recv, y_send, y_recv, a_send, a_recv, b_send, b_recv,
+    up_q_send, up_q_recv, down_send, down_recv, row_q_send, row_q_recv, back_send, back_recv,
+    dl_send, dl_recv, s1_send, s1_recv, s5_send, s5_recv, one_send, one_recv,
 ):
     nz = size // 4
     here = lax.axis_index("seq")
@@ -102,8 +109,14 @@
     tq = min(256, length)
     has_z = z > 0
     has_next = z < nz - 1
-    has_y = has_z | (row == 1)
-    has_b = has_z | (core == 1)
+    assert heads % nz == 0
+    share = heads // nz
+    slots = heads - share
+    served = share * (nz - 1 - z)
+    is_row0 = row == 0
+    below = jnp.where(is_row0 | (z == 0), share * (nz - z), share)
+    above = jnp.where(is_row0, served, jnp.where(has_next, share, 0))
+    swapped = jnp.maximum(above, share)
 
     def beside(d):
         r = 1 - row if d // 2 else row
@@ -141,94 +154,130 @@
 
     pl.semaphore_wait(barrier, 3 + jnp.minimum(z, 1) + jnp.minimum(nz - 1 - z, 1))
 
-    target = {Z: beyond(1), Y: beside(2), A: beside(1), B: beside(1)}
-
-    def side(kind, h, source):
+    halves = [(part, slice(0, length)) for part in range(2)]
+    piece = length // 4
+    pieces = [(part, slice(i * piece, (i + 1) * piece)) for part in range(2) for i in range(4)]
+
+    def y_head(t, to):
+        return jnp.where((to == 0) & (t < served), t, share + t)
+
+    def z_copy(t, n, cut):
+        part, rows = cut[n]
+        h = share + t
+        arrival = z_recv.at[t, n] if cut is halves else last_recv.at[n]
         return copy(
-            held.at[source, h], held.at[kind, h], side_send.at[kind - 1], side_recv.at[kind - 1, h],
-            target[kind],
+            (k_in, v_in)[part].at[rows, lanes_of(h)], held.at[Z, h, part, rows], z_send.at[t],
+            arrival, beyond(1),
         )
 
-    def arrived(kind, h):
-        side(kind, h, kind).wait_recv()
-
-    def all_sent(kind):
-        copy(
-            held.at[kind], held.at[kind], side_send.at[kind - 1], side_recv.at[kind - 1, 0],
-            target[kind],
-        ).wait_send()
-
-    piece = length // 4
-    halves = [(part, slice(0, length)) for part in range(2)]
-    pieces = [(part, slice(i * piece, (i + 1) * piece)) for part in range(2) for i in range(4)]
-
-    def z_copy(h, n, cut, arrival):
-        part, rows = cut[n]
+    def z_arrived(t, cut):
+        h = share + t
+
+        @pl.when(has_z & (h >= below))
+        def _():
+            for n, (part, rows) in enumerate(cut):
+                z_copy(t, n, cut).wait_recv()
+
+                @pl.when((row == 1) & (t >= served))
+                def _():
+                    copy(
+                        held.at[Z, h, part, rows], held.at[Y, h, part, rows], y_send.at[t],
+                        y_recv.at[t], beside(2),
+                    ).start()
+
+                @pl.when(core == 1)
+                def _():
+                    copy(
+                        held.at[Z, h, part, rows], held.at[B, h, part, rows], b_send.at[h],
+                        b_recv.at[h], beside(1),
+                    ).start()
+
+    def z_sent(t):
+        @pl.when(has_next & (share + t >= above))
+        def _():
+            copy(
+                held.at[Z, share + t], held.at[Z, share + t], z_send.at[t], z_recv.at[0, 0], beyond(1)
+            ).wait_send()
+
+    def z_offer(t, cut):
+        @pl.when(has_next & (share + t >= above))
+        def _():
+            for n in range(len(cut)):
+                z_copy(t, n, cut).start()
+
+    def y_all(t):
+        h = y_head(t, row)
+        return copy(held.at[Y, h], held.at[Y, h], y_send.at[t], y_recv.at[t], beside(2))
+
+    def a_all(t):
+        h = y_head(t, row)
+        return copy(held.at[Y, h], held.at[A, h], a_send, a_recv.at[t], beside(1))
+
+    def b_all(h):
+        return copy(held.at[B, h], held.at[B, h], b_send.at[h], b_recv.at[h], beside(1))
+
+    def b_own(h):
+        for part, ref in ((0, k_in), (1, v_in)):
+            copy(
+                ref.at[:, lanes_of(h)], held.at[B, h, part], b_send.at[h], b_recv.at[h], beside(1)
+            ).start()
+
+    def to_below(h):
         return copy(
-            (k_in, v_in)[part].at[rows, lanes_of(h)], held.at[Z, h, part, rows], z_send.at[h],
-            arrival(n), target[Z],
+            q_in.at[:, lanes_of(h)], up_q.at[h], up_q_send.at[h], up_q_recv.at[h], beyond(-1)
         )
 
-    def z_relay(h, n, cut, kind):
-        part, rows = cut[n]
+    def to_above(h):
+        return (
+            copy(down_o.at[h], up_o.at[h], down_send.at[h, 0], down_recv.at[h, 0], beyond(1)),
+            copy(down_s.at[h], up_s.at[h], down_send.at[h, 1], down_recv.at[h, 1], beyond(1)),
+        )
+
+    def ask_row(h):
         return copy(
-            held.at[Z, h, part, rows], held.at[kind, h, part, rows], side_send.at[kind - 1],
-            side_recv.at[kind - 1, h], target[kind],
+            q_in.at[:, lanes_of(h)], row_q.at[h], row_q_send.at[h], row_q_recv.at[h], beside(2)
         )
 
-    def first_sems(n):
-        return edge_recv.at[0, n]
-
-    def last_sems(n):
-        return edge_recv.at[1, n]
-
-    def z_arrived(h, n, cut, arrival):
-        @pl.when(has_z)
-        def _():
-            z_copy(h, n, cut, arrival).wait_recv()
-
-            @pl.when(row == 1)
-            def _():
-                z_relay(h, n, cut, Y).start()
-
-            @pl.when(core == 1)
-            def _():
-                z_relay(h, n, cut, B).start()
-
-    def z_sent(h):
-        copy(
-            held.at[Z, h], held.at[Z, h], z_send.at[h], z_recv.at[h, 0], target[Z]
-        ).wait_send()
-
-    def z_offer(h, cut, arrival):
-        @pl.when(has_next)
-        def _():
-            for n in range(len(cut)):
-                z_copy(h, n, cut, arrival).start()
-
-    def side_offer(h):
-        def send_own(kind):
+    def answer_row(h):
+        return (
+            copy(back_o.at[h], row_o.at[h], back_send.at[h, 0], back_recv.at[h, 0], beside(2)),
+            copy(back_s.at[h], row_s.at[h], back_send.at[h, 1], back_recv.at[h, 1], beside(2)),
+        )
+
+    def side_offer(t):
+        @pl.when((row == 1) & (t < share))
+        def _():
+            ask_row(t).start()
+
+        @pl.when((row == 0) | (t < served))
+        def _():
+            h = y_head(t, 1 - row)
             for part, ref in ((0, k_in), (1, v_in)):
                 copy(
-                    ref.at[:, lanes_of(h)], held.at[kind, h, part], side_send.at[kind - 1],
-                    side_recv.at[kind - 1, h], target[kind],
+                    ref.at[:, lanes_of(h)], held.at[Y, h, part], y_send.at[t], y_recv.at[t],
+                    beside(2),
                 ).start()
 
-        @pl.when(row == 0)
-        def _():
-            send_own(Y)
-
         @pl.when(core == 0)
         def _():
-            send_own(B)
-
-    def z_sems(h):
-        return lambda n: z_recv.at[h, n]
-
-    z_offer(0, pieces, first_sems)
+            b_own(share + t)
+
+        @pl.when(((core == 0) & (t < share)) | ((core == 1) & (t < swapped)))
+        def _():
+            b_own(t)
+
+    shift = jnp.where(has_next, above - share, 0)
+    z_offer(shift, halves)
     side_offer(0)
-    z_offer(1, halves, z_sems(1))
-    side_offer(1)
+
+    @pl.when(has_z)
+    def _():
+        def ask(h, carry):
+            to_below(h).start()
+            return carry
+
+        lax.fori_loop(0, below, ask, 0)
+
     for one in loads[6:]:
         one.start()
 
@@ -358,63 +407,181 @@
                 entry = entry * dec[b : b + 1, cs] + local[b, :, cs]
         return carry
 
-    def off(seen):
-        return jnp.where(seen, 0.0, NEG).astype(F32)
-
-    bias = {Z: off(has_z), Y: off(has_y), A: off(has_y), B: off(has_b)}
-
-    def keep(rows, m, l, acc):
-        acc_ref[rows, :] = acc
-        ml_ref[0, rows, :] = jnp.broadcast_to(m, acc.shape)
-        ml_ref[1, rows, :] = jnp.broadcast_to(l, acc.shape)
-
-    def more(h, kind, rows):
-        return flash(
-            q_ref[rows, lanes_of(h)], [(held[kind, h, 0], held[kind, h, 1], bias[kind], None)],
-            ml_ref[0, rows, 0:1], ml_ref[1, rows, 0:1], acc_ref[rows, :],
-        )
-
     query_rows = [slice(r, r + tq) for r in range(0, length, tq)]
 
-    def first_part(h):
+    def keep(slot, rows, m, l, acc):
+        acc_ref[slot, rows, :] = acc
+        ml_ref[slot, 0, rows, :] = m
+        ml_ref[slot, 1, rows, :] = l
+
+    def kept(slot, rows):
+        return ml_ref[slot, 0, rows, :], ml_ref[slot, 1, rows, :], acc_ref[slot, rows, :]
+
+    def held_tile(kind, h):
+        return (held[kind, h, 0], held[kind, h, 1], None)
+
+    def own_low(h, rows):
         hs = lanes_of(h)
+        tiles = [(k_ref[rows, hs], v_ref[rows, hs], "low")]
+        if rows.start > 0:
+            tiles.append((k_ref[0 : rows.start, hs], v_ref[0 : rows.start, hs], None))
+        return tiles
+
+    def own_up(h, rows):
+        hs = lanes_of(h)
+        tiles = [(k_ref[rows, hs], v_ref[rows, hs], "up")]
+        if rows.stop < length:
+            tiles.append((k_ref[rows.stop : length, hs], v_ref[rows.stop : length, hs], None))
+        return tiles
+
+    def z_up(h, rows):
+        tiles = [(held[Z, h, 0, rows, :], held[Z, h, 1, rows, :], "up")]
+        if rows.stop < length:
+            past = slice(rows.stop, length)
+            tiles.append((held[Z, h, 0, past, :], held[Z, h, 1, past, :], None))
+        return tiles
+
+    def begin(slot, q_of, tiles_of):
         for rows in query_rows:
-            tiles = [(k_ref[rows, hs], v_ref[rows, hs], None, "low")]
-            if rows.start > 0:
-                tiles.append((k_ref[0 : rows.start, hs], v_ref[0 : rows.start, hs], None, None))
-            tiles.append((held[Z, h, 0, rows, :], held[Z, h, 1, rows, :], bias[Z], "up"))
-            if rows.stop < length:
-                past = slice(rows.stop, length)
-                tiles.append((held[Z, h, 0, past, :], held[Z, h, 1, past, :], bias[Z], None))
-            tiles.append((held[B, h, 0], held[B, h, 1], bias[B], None))
-            keep(rows, *flash(q_ref[rows, hs], tiles, None, None, None))
-
-    def second_part(h):
+            keep(slot, rows, *flash(q_of(rows), tiles_of(rows), None, None, None))
+
+    def emit(m, l, acc, o_ref, s_ref, h, rows):
+        l = whole_sum(l)
+        o_ref[h, rows, :] = (acc / l).astype(BF16)
+        top = m + jnp.log(l) * LOG2E
+        s_ref[h, :, rows] = top.T[0:8, :]
+
+    def merge(slot, o_ref, s_ref, h):
         for rows in query_rows:
-            keep(rows, *more(h, Y, rows))
-
-    def third_part(h):
+            m, l, acc = kept(slot, rows)
+            top = jnp.concatenate([s_ref[h, :, rows]] * (LANES // 8), axis=0).T
+            m_new = jnp.maximum(m, top)
+            mine_part, their_part = jnp.exp2(m - m_new), jnp.exp2(top - m_new)
+            keep(
+                slot, rows, m_new, l * mine_part + jnp.where(lane == 0, their_part, 0.0),
+                acc * mine_part + o_ref[h, rows, :].astype(F32) * their_part,
+            )
+
+    def finish_head(slot, h):
         for rows in query_rows:
-            m, l, acc = more(h, A, rows)
-            attn_ref[rows, lanes_of(h)] = (acc / l).astype(attn_ref.dtype)
-
-    @pl.when(z == 0)
-    def _():
-        def clear(h, carry):
-            held[Z, h] = jnp.zeros(held.shape[2:], BF16)
-
-            @pl.when(row == 0)
-            def _():
-                held[Y, h] = jnp.zeros(held.shape[2:], BF16)
-                held[A, h] = jnp.zeros(held.shape[2:], BF16)
+            m, l, acc = kept(slot, rows)
+            attn_ref[rows, lanes_of(h)] = (acc / whole_sum(l)).astype(attn_ref.dtype)
+
+    def own_begin(slot, h):
+        def q_of(rows):
+            return q_ref[rows, lanes_of(h)]
+
+        @pl.when(core == 1)
+        def _():
+            begin(slot, q_of, lambda rows: own_low(h, rows) + [held_tile(B, h)])
+
+        @pl.when(core == 0)
+        def _():
+            begin(slot, q_of, lambda rows: own_low(h, rows))
+
+    def serving(t):
+        return is_row0 & (t < served)
+
+    def first_part(t):
+        @pl.when(serving(t))
+        def _():
+            to_below(t).wait_recv()
+            q_now[...] = up_q[t]
 
             @pl.when(core == 0)
             def _():
-                held[B, h] = jnp.zeros(held.shape[2:], BF16)
-
-            return carry
-
-        lax.fori_loop(0, heads, clear, 0)
+                begin(0, lambda rows: up_q[t, rows, :], lambda rows: own_up(t, rows) + [held_tile(B, t)])
+
+            @pl.when(core == 1)
+            def _():
+                begin(0, lambda rows: up_q[t, rows, :], lambda rows: own_up(t, rows))
+
+        @pl.when(jnp.logical_not(serving(t)))
+        def _():
+            h = share + t
+            q_now[...] = q_ref[:, lanes_of(h)]
+
+            @pl.when(has_z)
+            def _():
+                begin(
+                    0, lambda rows: q_ref[rows, lanes_of(h)],
+                    lambda rows: own_low(h, rows) + z_up(h, rows) + [held_tile(B, h)],
+                )
+
+            @pl.when(z == 0)
+            def _():
+                own_begin(0, h)
+
+    def second_part(t):
+        h = y_head(t, row)
+        rows = slice(0, length)
+        keep(0, rows, *flash(q_now[rows, :], [held_tile(Y, h)], *kept(0, rows)))
+
+    def third_part(t):
+        h = y_head(t, row)
+        rows = slice(0, length)
+        keep(0, rows, *flash(q_now[rows, :], [held_tile(A, h)], *kept(0, rows)))
+
+        @pl.when(serving(t))
+        def _():
+            for rows in query_rows:
+                emit(*kept(0, rows), down_o, down_s, t, rows)
+            for one in to_above(t):
+                one.start()
+
+        @pl.when(jnp.logical_not(serving(t)))
+        def _():
+            finish_head(0, h)
+
+    def serve_early(h):
+        @pl.when(is_row0)
+        def _():
+            ask_row(h).wait_recv()
+            hs = lanes_of(h)
+            for rows in query_rows:
+                own = (k_ref[:, hs], v_ref[:, hs], None)
+                result = flash(row_q[h, rows, :], [own, held_tile(B, h)], None, None, None)
+                emit(*result, back_o, back_s, h, rows)
+            for one in answer_row(h):
+                one.start()
+
+        @pl.when((row == 1) & has_next)
+        def _():
+            to_below(h).wait_recv()
+
+            def q_of(rows):
+                return up_q[h, rows, :]
+
+            @pl.when(core == 0)
+            def _():
+                begin(1, q_of, lambda rows: own_up(h, rows) + [held_tile(B, h)])
+
+            @pl.when(core == 1)
+            def _():
+                begin(1, q_of, lambda rows: own_up(h, rows))
+
+            for rows in query_rows:
+                emit(*kept(1, rows), down_o, down_s, h, rows)
+            for one in to_above(h):
+                one.start()
+
+    def light_head(h, carry):
+        own_begin(1, h)
+
+        @pl.when(row == 1)
+        def _():
+            for one in answer_row(h):
+                one.wait_recv()
+            merge(1, row_o, row_s, h)
+
+        @pl.when(has_z)
+        def _():
+            for one in to_above(h):
+                one.wait_recv()
+            merge(1, up_o, up_s, h)
+
+        finish_head(1, h)
+        return carry
 
     def decays(*which):
         for d in which:
@@ -455,12 +622,22 @@
             eout[...] = (near * far * entry + quad).astype(BF16)
             to_next().start()
 
-        s4out[...] = jnp.where(row == 0, near * entry + ours, entry).astype(BF16)
-        back_row().start()
+        @pl.when(has_z | is_row0)
+        def _():
+            s4out[...] = jnp.where(row == 0, near * entry + ours, entry).astype(BF16)
+            back_row().start()
+
+        @pl.when((z == 0) & is_row0)
+        def _():
+            ec[1] = jnp.zeros(ec.shape[1:], BF16)
+
         ec[row] = jnp.where(row == 0, entry, far * entry + theirs).astype(BF16)
 
     def pass_core():
-        back_row().wait_recv()
+        @pl.when(has_z | (row == 1))
+        def _():
+            back_row().wait_recv()
+
         for u in range(2):
             at = quarter(u, core)
             entry = ec[u].astype(F32)
@@ -470,17 +647,24 @@
             back_core(u).start()
             carried[:, at] = jnp.where(core == 0, entry, later).astype(BF16)
 
-    turn = jnp.minimum(2 + 2 * z, 8)
-    ready = turn + 2
-    fourth = pairs // 4
-
-    lax.fori_loop(0, pairs // 2, local_state, 0, unroll=4)
-    z_arrived(0, 0, pieces, first_sems)
-    lax.fori_loop(pairs // 2, pairs, local_state, 0, unroll=4)
+    turn = jnp.minimum(2 + (3 * z + 1) // 2, 7)
+    back = jnp.where(z < 2, turn + 2, turn + 1)
+    ready = back + 1
+    units = pairs // 2
+    lights = jnp.where(row == 1, share, below)
+
+    free = is_row0 & (z == 0)
+
+    def light_range(j):
+        count = jnp.where(j <= share, 2, 1)
+        count = jnp.where((j >= 1) & (j <= slots), count, 0)
+        first = jnp.clip(j - 3, 0, lights)
+        last = jnp.clip(j - 2, 0, lights)
+        return jnp.where(free, 0, first), jnp.where(free, count, last)
+
+    lax.fori_loop(0, pairs, local_state, 0, unroll=4)
     for u in range(2):
         to_core(u).start()
-    for n in range(1, len(pieces)):
-        z_arrived(0, n, pieces, first_sems)
     for one in loads[6:]:
         one.wait()
 
@@ -489,81 +673,98 @@
         def _():
             pass_state()
 
-        @pl.when((j < heads - 1) & (j >= 1))
-        def _():
-            for n in range(2):
-                z_arrived(j, n, halves, z_sems(j))
-
-        @pl.when(j == heads - 1)
-        def _():
-            for n in range(len(pieces)):
-                z_arrived(heads - 1, n, pieces, last_sems)
+        @pl.when(j < slots - 1)
+        def _():
+            z_arrived(j, halves)
+
+        @pl.when(j == slots - 1)
+        def _():
+            z_arrived(slots - 1, pieces)
 
         @pl.when(j == 0)
         def _():
             chip_totals()
-
-        @pl.when((j < heads) & has_next)
-        def _():
-            z_sent(j)
-
-        @pl.when(j + 2 < heads)
-        def _():
-            @pl.when(j + 3 < heads)
-            def _():
-                z_offer(j + 2, halves, z_sems(j + 2))
-
-            @pl.when(j + 3 == heads)
-            def _():
-                z_offer(heads - 1, pieces, last_sems)
-
+            z_offer(1 + shift, halves)
+            side_offer(1)
+
+        @pl.when((j >= 1) & (j <= slots))
+        def _():
+            @pl.when(j - 1 + shift < slots)
+            def _():
+                z_sent(j - 1 + shift)
+
+            @pl.when((row == 0) | (j - 1 < served))
+            def _():
+                y_all(j - 1).wait_send()
+
+        @pl.when(j + 3 + shift < slots)
+        def _():
+            z_offer(j + 2 + shift, halves)
+
+        @pl.when(j + 3 + shift == slots)
+        def _():
+            z_offer(slots - 1, pieces)
+
+        @pl.when(j + 2 < slots)
+        def _():
             side_offer(j + 2)
 
-        @pl.when(j >= 2)
-        def _():
-            @pl.when(has_y)
-            def _():
-                arrived(A, j - 2)
-
+        @pl.when((j >= 2) & (j < slots + 2))
+        def _():
+            a_all(j - 2).wait_recv()
             third_part(j - 2)
 
-        @pl.when((j >= 1) & (j <= heads))
-        def _():
-            @pl.when(has_b)
-            def _():
-                arrived(B, j - 1)
-
-            first_part(j - 1)
-
-            @pl.when(has_y)
-            def _():
-                arrived(Y, j - 1)
-                side(A, j - 1, Y).start()
-
-            second_part(j - 1)
-
-        @pl.when(j == turn + 1)
+        @pl.when((j >= 1) & (j <= slots))
+        def _():
+            t = j - 1
+
+            @pl.when((t < share) | ((core == 0) & (t < swapped)))
+            def _():
+                b_all(t).wait_recv()
+
+            @pl.when((core == 1) | (has_z & (share + t >= below)))
+            def _():
+                b_all(share + t).wait_recv()
+
+            @pl.when(t < share)
+            def _():
+                serve_early(t)
+
+            first_part(t)
+            y_all(t).wait_recv()
+            a_all(t).start()
+            second_part(t)
+
+        def light(i, carry):
+            waiting = jnp.where(i == 0, share + j - 1, j - 1)
+            return light_head(jnp.where(free, waiting, i), carry)
+
+        lax.fori_loop(*light_range(j), light, 0)
+
+        @pl.when(j == back)
         def _():
             pass_core()
 
-        @pl.when(j < pairs // 2)
-        def _():
-            for n in range(2):
-                intra(2 * j + n, 0)
-
-        @pl.when((j >= ready) & (j < ready + 4))
-        def _():
-            @pl.when(j == ready)
-            def _():
-                for u in range(2):
-                    back_core(u).wait_recv()
-
-            for n in range(fourth):
-                finish((j - ready) * fourth + n, 0)
+        @pl.when(j < 4)
+        def _():
+            for n in range(pairs // 4):
+                intra(pairs // 4 * j + n, 0)
+
+        @pl.when(j == ready)
+        def _():
+            for u in range(2):
+                back_core(u).wait_recv()
+
+        def finish_two(n, carry):
+            finish(2 * n, carry)
+            return finish(2 * n + 1, carry)
+
+        first = jnp.clip(3 * (j - ready), 0, units)
+        lax.fori_loop(first, jnp.clip(3 * (j - ready + 1), 0, units), finish_two, 0)
 
         return carry
 
-    lax.fori_loop(0, heads + 2, step, 0)
+    lax.fori_loop(0, slots + 3, step, 0)
 
     for d in range(1, 4):
         own_dl(d).wait_send()
@@ -571,23 +772,49 @@
         to_core(u).wait_send()
         back_core(u).wait_send()
     to_row().wait_send()
-    back_row().wait_send()
+
+    @pl.when(has_z | is_row0)
+    def _():
+        back_row().wait_send()
 
     @pl.when(has_next)
     def _():
         to_next().wait_send()
 
-    @pl.when(has_z | (row == 0))
-    def _():
-        all_sent(Y)
-
-    @pl.when(has_y)
-    def _():
-        all_sent(A)
-
-    @pl.when(has_z | (core == 0))
-    def _():
-        all_sent(B)
+    copy(
+        held.at[Y, pl.ds(0, slots)], held.at[A, pl.ds(0, slots)], a_send, a_recv.at[0], beside(1)
+    ).wait_send()
+
+    def drain(h, carry):
+        @pl.when((core == 0) | (h < swapped) | (has_z & (h >= below)))
+        def _():
+            b_all(h).wait_send()
+
+        @pl.when(has_z & (h < below))
+        def _():
+            to_below(h).wait_send()
+
+        @pl.when(has_next & (h < above))
+        def _():
+            for one in to_above(h):
+                one.wait_send()
+
+        @pl.when((h < slots) & (row == 1) & (h >= served))
+        def _():
+            y_all(h).wait_send()
+
+        @pl.when((h < share) & (row == 1))
+        def _():
+            ask_row(h).wait_send()
+
+        @pl.when((h < share) & (row == 0))
+        def _():
+            for one in answer_row(h):
+                one.wait_send()
+
+        return carry
+
+    lax.fori_loop(0, heads, drain, 0)
 
 
 def on_device(queries, keys, values, ssd_input, bmat, cmat, expo, rate, skip):
@@ -599,6 +826,8 @@
     heads = total_cols // E
     blocks = length // Q
     group = x_cols // 4
+    share = heads // (size // 4)
+    slots = heads - share
     vmem = pl.BlockSpec(memory_space=pltpu.VMEM)
     dma = pltpu.SemaphoreType.DMA
     inputs = (
@@ -637,14 +866,37 @@
             pltpu.VMEM((2, state, group), BF16),
             pltpu.VMEM((state, x_cols), BF16),
             pltpu.VMEM((length, x_cols), F32),
-            pltpu.VMEM((length, E), F32),
             pltpu.VMEM((2, length, E), F32),
+            pltpu.VMEM((2, 2, length, E), F32),
+            pltpu.VMEM((length, E), BF16),
+            pltpu.VMEM((heads, length, E), BF16),
+            pltpu.VMEM((heads, length, E), BF16),
+            pltpu.VMEM((heads, 8, length), F32),
+            pltpu.VMEM((heads, length, E), BF16),
+            pltpu.VMEM((heads, 8, length), F32),
+            pltpu.VMEM((share, length, E), BF16),
+            pltpu.VMEM((share, length, E), BF16),
+            pltpu.VMEM((share, 8, length), F32),
+            pltpu.VMEM((share, length, E), BF16),
+            pltpu.VMEM((share, 8, length), F32),
             dma((9,)),
+            dma((slots,)),
+            dma((slots, 2)),
+            dma((8,)),
+            dma((slots,)),
+            dma((slots,)),
+            dma,
+            dma((slots,)),
+            dma((heads,)),
+            dma((heads,)),
+            dma((heads,)),
             dma((heads,)),
             dma((heads, 2)),
-            dma((2, 8)),
-            dma((3,)),
-            dma((3, heads)),
+            dma((heads, 2)),
+            dma((share,)),
+            dma((share,)),
+            dma((share, 2)),
+            dma((share, 2)),
             dma((4,)),
             dma((4,)),
             dma((2,)),

time: 113 us -> 108 us (0.956)
  Pallas kernels: 109 us -> 104 us
    pallas_call x1, Pallas kernels: 109 us -> 104 us  [on_device(): pl.pallas_call(functools.partial(kernel, size), in_specs=[pl.BlockSpec(me...]
where the time goes in v4:
time: 108 us
  Pallas kernels  104 us (96%)
  local copies, waits for them, and re-layouts  2.64 us (2%)
    pallas_call x1, Pallas kernels, on_device(): pl.pallas_call(functools.partial(kernel, size), in_specs=[pl.BlockSpec(me...  104 us
    unnamed x2, local copies, waits for them, and re-layouts  2.64 us

profile of v4, /device:TPU:9, one launch (start us, length us, event | category | flops | bytes accessed | tf_op | source)
XLA Modules:
  0.0 107.6 jit_solution(15784259627557007815)
XLA Ops:
  0.6 104.3 %attention_and_recurrence.1 = (bf16[512,2048]{1,0:T(8,128)(2,1)S(1)}, bf16[512,2048]{1,0:T(8,128)(2,1)S(1)}) custom-call(bf16[512,2048]{1,0:T(8,128)(2,1)} %q_in.1, bf16[512,2048]{1,0:T(8,128)(2,1)} %k_in.1, bf16[512,2048]{1,0:T(8,128)(2,1)} %v_in.1, bf16[512,2048]{1,0:T(8,128)(2,1)} %x_in.1, bf16[512,128]{1,0:T(8,128)(2,1)} %b_in.1, bf16[512,128]{1,0:T(8,128)(2,1)} %c_in.1, ...), custom_call_target="tpu_custom_call" | custom-call | tf_op jit(solution)/shard_map/attention_and_recurrence/pallas_call | solution.py:837
  104.9 1.3 %copy.13 = bf16[512,2048]{1,0:T(8,128)(2,1)} copy(bf16[512,2048]{1,0:T(8,128)(2,1)S(1)} %get-tuple-element.4) | data formatting | bytes 4194304
  106.3 1.3 %copy.14 = bf16[512,2048]{1,0:T(8,128)(2,1)} copy(bf16[512,2048]{1,0:T(8,128)(2,1)S(1)} %get-tuple-element.5) | data formatting | bytes 4194304

commit v5 on v4

--- a/solution.py
+++ b/solution.py
@@ -88,7 +88,7 @@
     cross, dec, skx, dl, dtab, local, tot, s1, tc, s2, ein, eout, s4out, ec, s5out, carried, mixed,
     acc_ref, ml_ref, q_now, up_q, up_o, up_s, down_o, down_s, row_q, row_o, row_s, back_o, back_s,
     load, z_send, z_recv, last_recv, y_send, y_recv, a_send, a_recv, b_send, b_recv,
-    up_q_send, up_q_recv, down_send, down_recv, row_q_send, row_q_recv, back_send, back_recv,
+    y_relay_send, up_q_send, up_q_recv, down_send, down_recv, row_q_send, row_q_recv, back_send, back_recv,
     dl_send, dl_recv, s1_send, s1_recv, s5_send, s5_recv, one_send, one_recv,
 ):
     nz = size // 4
@@ -154,6 +154,9 @@
 
     pl.semaphore_wait(barrier, 3 + jnp.minimum(z, 1) + jnp.minimum(nz - 1 - z, 1))
 
+    def team(h):
+        return lax.div(h, share)
+
     halves = [(part, slice(0, length)) for part in range(2)]
     piece = length // 4
     pieces = [(part, slice(i * piece, (i + 1) * piece)) for part in range(2) for i in range(4)]
@@ -181,14 +184,14 @@
                 @pl.when((row == 1) & (t >= served))
                 def _():
                     copy(
-                        held.at[Z, h, part, rows], held.at[Y, h, part, rows], y_send.at[t],
-                        y_recv.at[t], beside(2),
+                        held.at[Z, h, part, rows], held.at[Y, h, part, rows],
+                        y_relay_send.at[team(t)], y_recv.at[t], beside(2),
                     ).start()
 
                 @pl.when(core == 1)
                 def _():
                     copy(
-                        held.at[Z, h, part, rows], held.at[B, h, part, rows], b_send.at[h],
+                        held.at[Z, h, part, rows], held.at[B, h, part, rows], b_send.at[team(h)],
                         b_recv.at[h], beside(1),
                     ).start()
 
@@ -214,34 +217,35 @@
         return copy(held.at[Y, h], held.at[A, h], a_send, a_recv.at[t], beside(1))
 
     def b_all(h):
-        return copy(held.at[B, h], held.at[B, h], b_send.at[h], b_recv.at[h], beside(1))
+        return copy(held.at[B, h], held.at[B, h], b_send.at[0], b_recv.at[h], beside(1))
 
     def b_own(h):
         for part, ref in ((0, k_in), (1, v_in)):
             copy(
-                ref.at[:, lanes_of(h)], held.at[B, h, part], b_send.at[h], b_recv.at[h], beside(1)
+                ref.at[:, lanes_of(h)], held.at[B, h, part], b_send.at[team(h)], b_recv.at[h],
+                beside(1),
             ).start()
 
     def to_below(h):
         return copy(
-            q_in.at[:, lanes_of(h)], up_q.at[h], up_q_send.at[h], up_q_recv.at[h], beyond(-1)
+            q_in.at[:, lanes_of(h)], up_q.at[h], up_q_send.at[team(h)], up_q_recv.at[h], beyond(-1)
         )
 
     def to_above(h):
         return (
-            copy(down_o.at[h], up_o.at[h], down_send.at[h, 0], down_recv.at[h, 0], beyond(1)),
-            copy(down_s.at[h], up_s.at[h], down_send.at[h, 1], down_recv.at[h, 1], beyond(1)),
+            copy(down_o.at[h], up_o.at[h], down_send.at[team(h), 0], down_recv.at[h, 0], beyond(1)),
+            copy(down_s.at[h], up_s.at[h], down_send.at[team(h), 1], down_recv.at[h, 1], beyond(1)),
         )
 
     def ask_row(h):
         return copy(
-            q_in.at[:, lanes_of(h)], row_q.at[h], row_q_send.at[h], row_q_recv.at[h], beside(2)
+            q_in.at[:, lanes_of(h)], row_q.at[h], row_q_send, row_q_recv.at[h], beside(2)
         )
 
     def answer_row(h):
         return (
-            copy(back_o.at[h], row_o.at[h], back_send.at[h, 0], back_recv.at[h, 0], beside(2)),
-            copy(back_s.at[h], row_s.at[h], back_send.at[h, 1], back_recv.at[h, 1], beside(2)),
+            copy(back_o.at[h], row_o.at[h], back_send.at[0], back_recv.at[h, 0], beside(2)),
+            copy(back_s.at[h], row_s.at[h], back_send.at[1], back_recv.at[h, 1], beside(2)),
         )
 
     def side_offer(t):
@@ -452,7 +456,7 @@
         s_ref[h, :, rows] = top.T[0:8, :]
 
     def merge(slot, o_ref, s_ref, h):
-        for rows in query_rows:
+        for rows in [slice(0, length)]:
             m, l, acc = kept(slot, rows)
             top = jnp.concatenate([s_ref[h, :, rows]] * (LANES // 8), axis=0).T
             m_new = jnp.maximum(m, top)
@@ -463,21 +467,21 @@
             )
 
     def finish_head(slot, h):
-        for rows in query_rows:
+        for rows in [slice(0, length)]:
             m, l, acc = kept(slot, rows)
             attn_ref[rows, lanes_of(h)] = (acc / whole_sum(l)).astype(attn_ref.dtype)
 
+    def extend(slot, q, tile):
+        rows = slice(0, length)
+        keep(slot, rows, *flash(q, [tile], *kept(slot, rows)))
+
     def own_begin(slot, h):
-        def q_of(rows):
-            return q_ref[rows, lanes_of(h)]
+        hs = lanes_of(h)
+        begin(slot, lambda rows: q_ref[rows, hs], lambda rows: own_low(h, rows))
 
         @pl.when(core == 1)
         def _():
-            begin(slot, q_of, lambda rows: own_low(h, rows) + [held_tile(B, h)])
-
-        @pl.when(core == 0)
-        def _():
-            begin(slot, q_of, lambda rows: own_low(h, rows))
+            extend(slot, q_ref[:, hs], held_tile(B, h))
 
     def serving(t):
         return is_row0 & (t < served)
@@ -488,13 +492,11 @@
             to_below(t).wait_recv()
             q_now[...] = up_q[t]
 
+            begin(0, lambda rows: up_q[t, rows, :], lambda rows: own_up(t, rows))
+
             @pl.when(core == 0)
             def _():
-                begin(0, lambda rows: up_q[t, rows, :], lambda rows: own_up(t, rows) + [held_tile(B, t)])
-
-            @pl.when(core == 1)
-            def _():
-                begin(0, lambda rows: up_q[t, rows, :], lambda rows: own_up(t, rows))
+                extend(0, up_q[t], held_tile(B, t))
 
         @pl.when(jnp.logical_not(serving(t)))
         def _():
@@ -505,8 +507,9 @@
             def _():
                 begin(
                     0, lambda rows: q_ref[rows, lanes_of(h)],
-                    lambda rows: own_low(h, rows) + z_up(h, rows) + [held_tile(B, h)],
+                    lambda rows: own_low(h, rows) + z_up(h, rows),
                 )
+                extend(0, q_ref[:, lanes_of(h)], held_tile(B, h))
 
             @pl.when(z == 0)
             def _():
@@ -524,7 +527,7 @@
 
         @pl.when(serving(t))
         def _():
-            for rows in query_rows:
+            for rows in [slice(0, length)]:
                 emit(*kept(0, rows), down_o, down_s, t, rows)
             for one in to_above(t):
                 one.start()
@@ -538,10 +541,9 @@
         def _():
             ask_row(h).wait_recv()
             hs = lanes_of(h)
-            for rows in query_rows:
-                own = (k_ref[:, hs], v_ref[:, hs], None)
-                result = flash(row_q[h, rows, :], [own, held_tile(B, h)], None, None, None)
-                emit(*result, back_o, back_s, h, rows)
+            own = (k_ref[:, hs], v_ref[:, hs], None)
+            result = flash(row_q[h], [own, held_tile(B, h)], None, None, None)
+            emit(*result, back_o, back_s, h, slice(0, length))
             for one in answer_row(h):
                 one.start()
 
@@ -549,18 +551,13 @@
         def _():
             to_below(h).wait_recv()
 
-            def q_of(rows):
-                return up_q[h, rows, :]
+            begin(1, lambda rows: up_q[h, rows, :], lambda rows: own_up(h, rows))
 
             @pl.when(core == 0)
             def _():
-                begin(1, q_of, lambda rows: own_up(h, rows) + [held_tile(B, h)])
-
-            @pl.when(core == 1)
-            def _():
-                begin(1, q_of, lambda rows: own_up(h, rows))
-
-            for rows in query_rows:
+                extend(1, up_q[h], held_tile(B, h))
+
+            for rows in [slice(0, length)]:
                 emit(*kept(1, rows), down_o, down_s, h, rows)
             for one in to_above(h):
                 one.start()
@@ -785,36 +782,41 @@
         held.at[Y, pl.ds(0, slots)], held.at[A, pl.ds(0, slots)], a_send, a_recv.at[0], beside(1)
     ).wait_send()
 
-    def drain(h, carry):
-        @pl.when((core == 0) | (h < swapped) | (has_z & (h >= below)))
-        def _():
-            b_all(h).wait_send()
-
-        @pl.when(has_z & (h < below))
-        def _():
-            to_below(h).wait_send()
-
-        @pl.when(has_next & (h < above))
-        def _():
-            for one in to_above(h):
-                one.wait_send()
-
-        @pl.when((h < slots) & (row == 1) & (h >= served))
-        def _():
-            y_all(h).wait_send()
-
-        @pl.when((h < share) & (row == 1))
-        def _():
-            ask_row(h).wait_send()
-
-        @pl.when((h < share) & (row == 0))
-        def _():
-            for one in answer_row(h):
-                one.wait_send()
+    def left(ref, sender):
+        copy(ref, ref, sender, up_q_recv.at[0], beside(1)).wait_send()
+
+    def drain(g, carry):
+        some = pl.ds(g * share, share)
+
+        @pl.when((core == 0) | (g * share < swapped) | (has_z & (g * share >= below)))
+        def _():
+            left(held.at[B, some], b_send.at[g])
+
+        @pl.when(has_z & (g * share < below))
+        def _():
+            left(up_q.at[some], up_q_send.at[g])
+
+        @pl.when(has_next & (g * share < above))
+        def _():
+            left(down_o.at[some], down_send.at[g, 0])
+            left(down_s.at[some], down_send.at[g, 1])
+
+        @pl.when((g * share < slots) & (row == 1) & (g * share >= served))
+        def _():
+            left(held.at[Y, some], y_relay_send.at[g])
 
         return carry
 
-    lax.fori_loop(0, heads, drain, 0)
+    lax.fori_loop(0, nz, drain, 0)
+
+    @pl.when(row == 1)
+    def _():
+        left(row_q, row_q_send)
+
+    @pl.when(row == 0)
+    def _():
+        left(back_o, back_send.at[0])
+        left(back_s, back_send.at[1])
 
 
 def on_device(queries, keys, values, ssd_input, bmat, cmat, expo, rate, skip):
@@ -887,15 +889,16 @@
             dma((slots,)),
             dma,
             dma((slots,)),
+            dma((heads // share,)),
             dma((heads,)),
+            dma((heads // share,)),
+            dma((heads // share,)),
             dma((heads,)),
-            dma((heads,)),
-            dma((heads,)),
+            dma((heads // share, 2)),
             dma((heads, 2)),
-            dma((heads, 2)),
+            dma,
             dma((share,)),
-            dma((share,)),
-            dma((share, 2)),
+            dma((2,)),
             dma((share, 2)),
             dma((4,)),
             dma((4,)),

time: 108 us -> 106 us (0.981)
  Pallas kernels: 104 us -> 102 us
    pallas_call x1, Pallas kernels: 104 us -> 102 us  [on_device(): pl.pallas_call(functools.partial(kernel, size), in_specs=[pl.BlockSpec(me...]
where the time goes in v5:
time: 106 us
  Pallas kernels  102 us (96%)
  local copies, waits for them, and re-layouts  2.64 us (2%)
    pallas_call x1, Pallas kernels, on_device(): pl.pallas_call(functools.partial(kernel, size), in_specs=[pl.BlockSpec(me...  102 us
    unnamed x2, local copies, waits for them, and re-layouts  2.64 us

profile of v5, /device:TPU:9, one launch (start us, length us, event | category | flops | bytes accessed | tf_op | source)
XLA Modules:
  0.0 105.6 jit_solution(9040585521967291578)
XLA Ops:
  0.6 102.4 %attention_and_recurrence.1 = (bf16[512,2048]{1,0:T(8,128)(2,1)S(1)}, bf16[512,2048]{1,0:T(8,128)(2,1)S(1)}) custom-call(bf16[512,2048]{1,0:T(8,128)(2,1)} %q_in.1, bf16[512,2048]{1,0:T(8,128)(2,1)} %k_in.1, bf16[512,2048]{1,0:T(8,128)(2,1)} %v_in.1, bf16[512,2048]{1,0:T(8,128)(2,1)} %x_in.1, bf16[512,128]{1,0:T(8,128)(2,1)} %b_in.1, bf16[512,128]{1,0:T(8,128)(2,1)} %c_in.1, ...), custom_call_target="tpu_custom_call" | custom-call | tf_op jit(solution)/shard_map/attention_and_recurrence/pallas_call | solution.py:839
  103.0 1.3 %copy.13 = bf16[512,2048]{1,0:T(8,128)(2,1)} copy(bf16[512,2048]{1,0:T(8,128)(2,1)S(1)} %get-tuple-element.4) | data formatting | bytes 4194304
  104.3 1.3 %copy.14 = bf16[512,2048]{1,0:T(8,128)(2,1)} copy(bf16[512,2048]{1,0:T(8,128)(2,1)S(1)} %get-tuple-element.5) | data formatting | bytes 4194304

commit v6 on v5

--- a/solution.py
+++ b/solution.py
@@ -75,6 +75,34 @@
             l = l * alpha + total
             acc = acc * alpha + part
         m = m_new
+    return m, l, acc
+
+
+def attend(q, tiles):
+    tq = q.shape[0]
+    scale = LOG2E / math.sqrt(E)
+    low = iota((tq, tq), 1) <= iota((tq, tq), 0)
+    scores = []
+    for k, v, mask in tiles:
+        s = dot_t(q, k) * scale
+        if isinstance(mask, tuple):
+            s = jnp.where(low, s, dot_t(q, mask[0]) * scale)
+        elif mask is not None:
+            s = jnp.where(low, s, NEG) if mask == "low" else jnp.where(low, NEG, s)
+        scores.append(s)
+    peak = functools.reduce(jnp.maximum, [jnp.max(s, axis=1, keepdims=True) for s in scores])
+    m = jnp.broadcast_to(peak, (tq, LANES))
+    l = acc = 0.0
+    for s, (k, v, mask) in zip(scores, tiles):
+        groups = s.shape[1] // LANES
+        p = jnp.exp2(s - jnp.concatenate([m] * groups, axis=1))
+        for g in range(groups):
+            l = l + p[:, g * LANES : (g + 1) * LANES]
+        if isinstance(mask, tuple):
+            acc = acc + dot(jnp.where(low, p, 0.0).astype(BF16), v)
+            acc = acc + dot(jnp.where(low, 0.0, p).astype(BF16), mask[1])
+        else:
+            acc = acc + dot(p.astype(BF16), v)
     return m, l, acc
 
 
@@ -438,8 +466,12 @@
             tiles.append((k_ref[rows.stop : length, hs], v_ref[rows.stop : length, hs], None))
         return tiles
 
-    def z_up(h, rows):
-        tiles = [(held[Z, h, 0, rows, :], held[Z, h, 1, rows, :], "up")]
+    def own_and_z(h, rows):
+        hs = lanes_of(h)
+        z_k, z_v = held[Z, h, 0, rows, :], held[Z, h, 1, rows, :]
+        tiles = [(k_ref[rows, hs], v_ref[rows, hs], (z_k, z_v))]
+        if rows.start > 0:
+            tiles.append((k_ref[0 : rows.start, hs], v_ref[0 : rows.start, hs], None))
         if rows.stop < length:
             past = slice(rows.stop, length)
             tiles.append((held[Z, h, 0, past, :], held[Z, h, 1, past, :], None))
@@ -447,7 +479,7 @@
 
     def begin(slot, q_of, tiles_of):
         for rows in query_rows:
-            keep(slot, rows, *flash(q_of(rows), tiles_of(rows), None, None, None))
+            keep(slot, rows, *attend(q_of(rows), tiles_of(rows)))
 
     def emit(m, l, acc, o_ref, s_ref, h, rows):
         l = whole_sum(l)
@@ -507,7 +539,7 @@
             def _():
                 begin(
                     0, lambda rows: q_ref[rows, lanes_of(h)],
-                    lambda rows: own_low(h, rows) + z_up(h, rows),
+                    lambda rows: own_and_z(h, rows),
                 )
                 extend(0, q_ref[:, lanes_of(h)], held_tile(B, h))
 
@@ -649,14 +681,19 @@
     ready = back + 1
     units = pairs // 2
     lights = jnp.where(row == 1, share, below)
+    lag = 3
+
+    def light_count(j):
+        soon = jnp.where(j > slots // 2 + 2, j - 2, j - 3)
+        return jnp.clip(jnp.where(is_row0 & (z == 1), soon, j - lag), 0, lights)
+
 
     free = is_row0 & (z == 0)
 
     def light_range(j):
         count = jnp.where(j <= share, 2, 1)
         count = jnp.where((j >= 1) & (j <= slots), count, 0)
-        first = jnp.clip(j - 3, 0, lights)
-        last = jnp.clip(j - 2, 0, lights)
+        first, last = light_count(j), light_count(j + 1)
         return jnp.where(free, 0, first), jnp.where(free, count, last)
 
     lax.fori_loop(0, pairs, local_state, 0, unroll=4)
@@ -665,7 +702,35 @@
     for one in loads[6:]:
         one.wait()
 
+    def left(ref, sender):
+        copy(ref, ref, sender, up_q_recv.at[0], beside(1)).wait_send()
+
+    def drain_early():
+        for d in range(1, 4):
+            own_dl(d).wait_send()
+        for u in range(2):
+            to_core(u).wait_send()
+        to_row().wait_send()
+        for g in range(nz):
+
+            @pl.when(has_z & (g * share < below))
+            def _():
+                left(up_q.at[g * share : (g + 1) * share], up_q_send.at[g])
+
+        @pl.when(row == 1)
+        def _():
+            left(row_q, row_q_send)
+
+        @pl.when(row == 0)
+        def _():
+            left(back_o, back_send.at[0])
+            left(back_s, back_send.at[1])
+
     def step(j, carry):
+        @pl.when(j == slots - 2)
+        def _():
+            drain_early()
+
         @pl.when(j == turn)
         def _():
             pass_state()
@@ -761,14 +826,10 @@
 
         return carry
 
-    lax.fori_loop(0, slots + 3, step, 0)
-
-    for d in range(1, 4):
-        own_dl(d).wait_send()
+    lax.fori_loop(0, slots + 2, step, 0)
+
     for u in range(2):
-        to_core(u).wait_send()
         back_core(u).wait_send()
-    to_row().wait_send()
 
     @pl.when(has_z | is_row0)
     def _():
@@ -782,9 +843,6 @@
         held.at[Y, pl.ds(0, slots)], held.at[A, pl.ds(0, slots)], a_send, a_recv.at[0], beside(1)
     ).wait_send()
 
-    def left(ref, sender):
-        copy(ref, ref, sender, up_q_recv.at[0], beside(1)).wait_send()
-
     def drain(g, carry):
         some = pl.ds(g * share, share)
 
@@ -792,10 +850,6 @@
         def _():
             left(held.at[B, some], b_send.at[g])
 
-        @pl.when(has_z & (g * share < below))
-        def _():
-            left(up_q.at[some], up_q_send.at[g])
-
         @pl.when(has_next & (g * share < above))
         def _():
             left(down_o.at[some], down_send.at[g, 0])
@@ -808,15 +862,6 @@
         return carry
 
     lax.fori_loop(0, nz, drain, 0)
-
-    @pl.when(row == 1)
-    def _():
-        left(row_q, row_q_send)
-
-    @pl.when(row == 0)
-    def _():
-        left(back_o, back_send.at[0])
-        left(back_s, back_send.at[1])
 
 
 def on_device(queries, keys, values, ssd_input, bmat, cmat, expo, rate, skip):

time: 106 us -> 104 us (0.981)
    pallas_call x1, Pallas kernels: 102 us -> 101 us  [on_device(): pl.pallas_call(functools.partial(kernel, size), in_specs=[pl.BlockSpec(me...]
where the time goes in v6:
time: 104 us
  Pallas kernels  101 us (97%)
  local copies, waits for them, and re-layouts  2.64 us (3%)
    pallas_call x1, Pallas kernels, on_device(): pl.pallas_call(functools.partial(kernel, size), in_specs=[pl.BlockSpec(me...  101 us
    unnamed x2, local copies, waits for them, and re-layouts  2.64 us

profile of v6, /device:TPU:9, one launch (start us, length us, event | category | flops | bytes accessed | tf_op | source)
XLA Modules:
  0.0 103.9 jit_solution(10314507123828541285)
XLA Ops:
  0.6 100.6 %attention_and_recurrence.1 = (bf16[512,2048]{1,0:T(8,128)(2,1)S(1)}, bf16[512,2048]{1,0:T(8,128)(2,1)S(1)}) custom-call(bf16[512,2048]{1,0:T(8,128)(2,1)} %q_in.1, bf16[512,2048]{1,0:T(8,128)(2,1)} %k_in.1, bf16[512,2048]{1,0:T(8,128)(2,1)} %v_in.1, bf16[512,2048]{1,0:T(8,128)(2,1)} %x_in.1, bf16[512,128]{1,0:T(8,128)(2,1)} %b_in.1, bf16[512,128]{1,0:T(8,128)(2,1)} %c_in.1, ...), custom_call_target="tpu_custom_call" | custom-call | tf_op jit(solution)/shard_map/attention_and_recurrence/pallas_call | solution.py:884
  101.2 1.3 %copy.13 = bf16[512,2048]{1,0:T(8,128)(2,1)} copy(bf16[512,2048]{1,0:T(8,128)(2,1)S(1)} %get-tuple-element.4) | data formatting | bytes 4194304
  102.5 1.3 %copy.14 = bf16[512,2048]{1,0:T(8,128)(2,1)} copy(bf16[512,2048]{1,0:T(8,128)(2,1)S(1)} %get-tuple-element.5) | data formatting | bytes 4194304
